TPU v7x, 256 devices: a whole 4x4x8 slice. The times are simulated.
256 devices in a mesh: row: 16 (over y, x), col: 16 (over z, core).
Axes of the slice: x: 4, y: 4, z: 8, core: 2. Of those that a mesh axis runs over, the one named last changes fastest.
Arguments:
- matrix: float32 [20480, 8, 2048], P('row', None, 'col'), may hold values from -36 to 36, as said below
Outputs:
- factors: float32 [20480, 8, 2048], P('row', None, 'col')
- upper: float32 [256, 8, 2048], P(None, None, 'col')
Inputs may be any that keep to these rules, and one draw needn't show every extreme that they name: A dense real matrix of full column rank.
All inputs are finite; a program needn't handle non-finite values.
Results may differ from a plain program's by a relative error of at most 0.0003.
Values sent between devices are 32-bit elements; how exact they have to be, the bound alone decides.
No kernel may reach another device: no remote copies, remote signals or barrier semaphores. Data moves between devices by JAX's collectives and lax.ppermute only.
A program may use at most 64 MiB of HBM per device.

v0:
```python
import math

import jax
import jax.numpy as jnp
from jax import lax
from jax.sharding import PartitionSpec as P


def spread(array, axis, root):
    mine = lax.axis_index(axis) == root
    return lax.psum(jnp.where(mine, array, jnp.zeros_like(array)), axis)


def upper_factor(gram):
    size = gram.shape[0]
    places = jnp.arange(size)

    def turn(j, carry):
        rest, lower = carry
        unit = (places == j).astype(gram.dtype)
        column = jnp.sum(rest * unit[None, :], axis=1)
        pivot = jnp.sqrt(jnp.sum(column * unit))
        column = jnp.where(places >= j, column / pivot, jnp.zeros_like(column))
        rest = rest - column[:, None] * column[None, :]
        lower = lower + column[:, None] * unit[None, :]
        return (rest, lower)

    rest, lower = lax.fori_loop(0, size, turn, (gram, jnp.zeros_like(gram)))
    return lower.T


def upper_inverse(factor):
    size = factor.shape[0]
    places = jnp.arange(size)

    def turn(step, inverse):
        j = size - 1 - step
        unit = (places == j).astype(factor.dtype)
        row_vals = jnp.sum(factor * unit[:, None], axis=0)
        pivot = jnp.sum(row_vals * unit)
        new_row = (unit - jnp.sum(row_vals[:, None] * inverse, axis=0)) / pivot
        return inverse + unit[:, None] * new_row[None, :]

    return lax.fori_loop(0, size, turn, jnp.zeros_like(factor))


def orthonormal(panel_rows):
    highest = lax.Precision.HIGHEST
    gram = jnp.dot(panel_rows.T, panel_rows, precision=highest, preferred_element_type=jnp.float32)
    factor = upper_factor(lax.psum(gram, "row"))
    return jnp.dot(
        panel_rows, upper_inverse(factor), precision=highest, preferred_element_type=jnp.float32
    )


def basis_for(block, spare, owner):
    source = jnp.where(lax.axis_index("col") == owner, block, spare)
    return spread(orthonormal(source), "col", owner)


def project(basis, work):
    local = jnp.einsum(
        "rp,rbc->pbc",
        basis,
        work,
        precision=lax.Precision.HIGHEST,
        preferred_element_type=jnp.float32,
    )
    return lax.psum(local, "row")


def remove(work, basis, coeffs):
    return work - jnp.einsum(
        "rp,pbc->rbc",
        basis,
        coeffs,
        precision=lax.Precision.HIGHEST,
        preferred_element_type=jnp.float32,
    )


def shards(matrix):
    scale = math.sqrt(matrix.shape[0] * lax.axis_size("row"))
    spare = matrix[:, 0, :]
    first = basis_for(matrix[:, 0, :], spare, 0)
    coef_one = project(first, matrix)
    middle = remove(matrix, first, coef_one)
    second = basis_for(middle[:, 0, :], spare, 1)
    coef_two = project(second, middle)
    final = remove(middle, second, coef_two)
    column = lax.axis_index("col")
    lead_block = jnp.where(
        column == 0, first * scale, jnp.where(column == 1, second * scale, final[:, 0, :])
    )
    factors = jnp.concatenate([lead_block[:, None, :], final[:, 1:, :]], axis=1)
    upper = jnp.concatenate([coef_one, coef_two], axis=0) / scale
    return (factors, upper)


def solution(mesh):
    in_specs = (P("row", None, "col"),)
    out_specs = (P("row", None, "col"), P(None, None, "col"))
    return jax.shard_map(shards, mesh=mesh, in_specs=in_specs, out_specs=out_specs, check_vma=False)
```

profile of v0, /device:TPU:2, one launch (start us, length us, event | category | flops | bytes accessed | tf_op | source)
XLA Modules:
  0.0 2057.2 jit_solution(17769544021011634935)
XLA Ops:
  7.2 6.2 copy.3
  13.4 2.6 fusion.26
  16.1 93.7 %all-reduce.7.cloned.1.call-done = f32[128,128]{1,0:T(8,128)} async-done(((f32[128,128]{1,0:T(8,128)}), f32[128,128]{1,0:T(8,128)}) %all-reduce.7.cloned.1.call-update) | async-done | bytes 65552 | tf_op jit(solution)/shard_map/psum | solution.py:50
  109.9 488.9 %while.64 = (s32[]{:T(128)}, f32[128,128]{1,0:T(8,128)}, f32[128,128]{1,0:T(8,128)S(1)}, s32[]{:T(128)}, s32[]{:T(128)}) while((s32[]{:T(128)}, f32[128,128]{1,0:T(8,128)}, f32[128,128]{1,0:T(8,128)S(1)}, s32[]{:T(128)}, s32[]{:T(128)}) %tuple.132), condition=%wide.region_4.5_spmd.clone.clone, body=%wide.region_1.4_spmd.clone.clone.sunk | while | flops 115586 | bytes 331883 | solution.py:28
  598.9 203.2 %while.62 = (s32[]{:T(128)}, f32[128,128]{1,0:T(8,128)S(1)}, f32[128,128]{1,0:T(8,128)S(1)}, s32[]{:T(128)}, s32[]{:T(128)}, /*index=5*/s32[]{:T(128)}) while((s32[]{:T(128)}, f32[128,128]{1,0:T(8,128)S(1)}, f32[128,128]{1,0:T(8,128)S(1)}, s32[]{:T(128)}, s32[]{:T(128)}, /*index=5*/s32[]{:T(128)}) %tuple.135), condition=%wide.region_9.10_spmd.clone, body=%wide.region_5.9_spmd.clone.sunk | while | flops 131971 | bytes 267384 | solution.py:44
  802.1 2.7 fusion.12
  804.9 110.1 %all-reduce.9.cloned.1.call-done = f32[1280,128]{0,1:T(8,128)} async-done(((f32[1280,128]{0,1:T(8,128)}), f32[1280,128]{0,1:T(8,128)}) %all-reduce.9.cloned.1.call-update) | async-done | bytes 655376 | tf_op jit(solution)/shard_map/psum | solution.py:11
  915.0 8.9 fusion.21
  924.0 95.3 %all-reduce.11.cloned.1.call-done = f32[128,8,128]{2,0,1:T(8,128)} async-done(((f32[128,8,128]{2,0,1:T(8,128)}), f32[128,8,128]{2,0,1:T(8,128)}) %all-reduce.11.cloned.1.call-update) | async-done | bytes 524304 | tf_op jit(solution)/shard_map/psum | solution.py:69
  1019.3 7.4 convolution_subtract_fusion.1
  1026.7 2.3 copy-done
  1029.0 2.6 fusion.19
  1031.9 90.4 %all-reduce.13.cloned.1.call-done = f32[128,128]{1,0:T(8,128)} async-done(((f32[128,128]{1,0:T(8,128)}), f32[128,128]{1,0:T(8,128)}) %all-reduce.13.cloned.1.call-update) | async-done | bytes 65552 | tf_op jit(solution)/shard_map/psum | solution.py:50
  1122.3 489.1 %while.65 = (s32[]{:T(128)}, f32[128,128]{1,0:T(8,128)}, f32[128,128]{1,0:T(8,128)S(1)}, s32[]{:T(128)}, s32[]{:T(128)}) while((s32[]{:T(128)}, f32[128,128]{1,0:T(8,128)}, f32[128,128]{1,0:T(8,128)S(1)}, s32[]{:T(128)}, s32[]{:T(128)}) %tuple.138), condition=%wide.region_16.17_spmd.clone.clone, body=%wide.region_13.16_spmd.clone.clone.sunk | while | flops 115586 | bytes 331883 | solution.py:28
  1128.4 1.6 select_add_fusion.5
  1611.5 203.2 %while.63 = (s32[]{:T(128)}, f32[128,128]{1,0:T(8,128)S(1)}, f32[128,128]{1,0:T(8,128)S(1)}, s32[]{:T(128)}, s32[]{:T(128)}, /*index=5*/s32[]{:T(128)}) while((s32[]{:T(128)}, f32[128,128]{1,0:T(8,128)S(1)}, f32[128,128]{1,0:T(8,128)S(1)}, s32[]{:T(128)}, s32[]{:T(128)}, /*index=5*/s32[]{:T(128)}) %tuple.141), condition=%wide.region_21.22_spmd.clone, body=%wide.region_17.21_spmd.clone.sunk | while | flops 131971 | bytes 267384 | solution.py:44
  1814.8 2.9 convolution_select_fusion
  1817.7 110.1 %all-reduce.15.cloned.1.call-done = f32[1280,128]{0,1:T(8,128)} async-done(((f32[1280,128]{0,1:T(8,128)}), f32[1280,128]{0,1:T(8,128)}) %all-reduce.15.cloned.1.call-update) | async-done | bytes 655376 | tf_op jit(solution)/shard_map/psum | solution.py:11
  1927.8 8.9 fusion.16
  1936.8 95.4 %all-reduce.17.cloned.1.call-done = f32[128,8,128]{2,0,1:T(8,128)} async-done(((f32[128,8,128]{2,0,1:T(8,128)}), f32[128,8,128]{2,0,1:T(8,128)}) %all-reduce.17.cloned.1.call-update) | async-done | bytes 524304 | tf_op jit(solution)/shard_map/psum | solution.py:69
  2032.1 7.0 convolution_subtract_fusion
  2039.7 2.7 pad_maximum_fusion
  2042.4 6.3 copy.14
  2048.8 1.6 copy.15
  (2845 shorter events, 1192.4 us)
Async XLA Ops:
  7.2 102.7 %all-reduce.7.cloned.1.call-start = ((), (), s32[]{:S(2)}) async-start(), calls=%async_computation | async-start | bytes 131072 | tf_op jit(solution)/shard_map/psum | solution.py:50
  16.1 898.9 %all-reduce.9.cloned.1.call-start = ((), (), s32[]{:S(2)}) async-start(), calls=%async_computation.1 | async-start | bytes 1310720 | tf_op jit(solution)/shard_map/psum | solution.py:11
  804.8 214.5 %all-reduce.11.cloned.1.call-start = ((), (), s32[]{:S(2)}) async-start(), calls=%async_computation.2 | async-start | bytes 1048576 | tf_op jit(solution)/shard_map/psum | solution.py:69
  915.0 104.3 %copy-start.1 = (f32[1280,128]{0,1:T(8,128)S(1)}, f32[1280,128]{0,1:T(8,128)}, u32[]{:S(2)}) copy-start(f32[1280,128]{0,1:T(8,128)} %all-reduce.9.cloned.1.call-done) | copy-start | bytes 1966084
  923.9 198.4 %all-reduce.13.cloned.1.call-start = ((), (), s32[]{:S(2)}) async-start(), calls=%async_computation.3 | async-start | bytes 131072 | tf_op jit(solution)/shard_map/psum | solution.py:50
  1026.7 2.3 copy-start
  1031.7 896.2 %all-reduce.15.cloned.1.call-start = ((), (), s32[]{:S(2)}) async-start(), calls=%async_computation.4 | async-start | bytes 1310720 | tf_op jit(solution)/shard_map/psum | solution.py:11
  1817.6 214.5 %all-reduce.17.cloned.1.call-start = ((), (), s32[]{:S(2)}) async-start(), calls=%async_computation.5 | async-start | bytes 1048576 | tf_op jit(solution)/shard_map/psum | solution.py:69
  1927.8 104.3 %copy-start.2 = (f32[1280,128]{0,1:T(8,128)S(1)}, f32[1280,128]{0,1:T(8,128)}, u32[]{:S(2)}) copy-start(f32[1280,128]{0,1:T(8,128)} %all-reduce.15.cloned.1.call-done) | copy-start | bytes 1966084
  2042.4 6.3 copy-start.3
  2042.4 6.3 copy-start.4
Sparse Core Ops, SparseCore 0:
  16.2 93.6 all-reduce.6
  804.9 110.0 all-reduce.8
  924.1 95.1 all-reduce.10
  1031.8 90.4 all-reduce.12
  1817.8 109.9 all-reduce.14
  1936.9 95.1 all-reduce.16
where the time goes:
time: 2090 us; the launch traced here: 2060 us
  other arithmetic  1200 us (57%)
  waiting for transfers between devices  595 us (28%)
  loops' own time  192 us (9%)
  matrix products  43 us (2%)
    add x256, other arithmetic, turn(): lower = lower + column[:, None] * unit[None, :]  398 us
    reduce_sum x256, other arithmetic, turn(): column = jnp.sum(rest * unit[None, :], axis=1)  241 us
    psum x2, waiting for transfers between devices, spread(): return lax.psum(jnp.where(mine, array, jnp.zeros_like(array)), axis)  220 us
    psum x2, waiting for transfers between devices, project(): return lax.psum(local, 'row')  191 us
    psum x2, waiting for transfers between devices, orthonormal(): factor = upper_factor(lax.psum(gram, 'row'))  184 us
    another operation x2, loops' own time, upper_factor(): rest, lower = lax.fori_loop(0, size, turn, (gram, jnp.zeros_like(gram)))  181 us
    div x256, other arithmetic, turn(): new_row = (unit - jnp.sum(row_vals[:, None] * inverse, axis=0)) / pivot  168 us
    reduce_sum x256, other arithmetic, turn(): pivot = jnp.sqrt(jnp.sum(column * unit))  157 us
  transfers between devices with their start and end apart: 6, of which 6 were waited for; matrix products, arithmetic and copies ran while one was open for 0% of the time, Pallas kernels for 0%

commit v1 on v0

v1 whole, which is shorter than its diff:
```python
import functools
import math

import jax
import jax.numpy as jnp
from jax import lax
from jax.experimental import pallas as pl
from jax.experimental.pallas import tpu as pltpu
from jax.sharding import PartitionSpec as P

F32 = jnp.float32
BF16 = jnp.bfloat16
HIGHEST = lax.Precision.HIGHEST
LANES = 128
SUB = 8


def split(x):
    high = x.astype(BF16)
    low = (x - high.astype(F32)).astype(BF16)
    return high, low


def dot3(a, b, dims=((1,), (0,))):
    mul = functools.partial(lax.dot_general, dimension_numbers=(dims, ((), ())), preferred_element_type=F32)
    return mul(a[0], b[0]) + (mul(a[0], b[1]) + mul(a[1], b[0]))


def dot6(a, b, dims=((1,), (0,))):
    return lax.dot_general(a, b, (dims, ((), ())), precision=HIGHEST, preferred_element_type=F32)


def gram_kernel(second_core, mine_ref, other_ref, m_ref, out_ref):
    rows = mine_ref.shape[0]
    blocks = m_ref.shape[0] // rows
    swapped = second_core[0] == 1
    mine, other = mine_ref[...], other_ref[...]
    panels = jnp.concatenate(
        [jnp.where(swapped, other, mine), jnp.where(swapped, mine, other)], axis=1
    )
    turned = panels.T
    left = split(turned)
    wide = blocks * LANES
    for k in range(0, blocks, 2):
        pair = jnp.concatenate(
            [m_ref[pl.ds(k, rows, stride=blocks), :], m_ref[pl.ds(k + 1, rows, stride=blocks), :]], axis=1
        )
        out_ref[:, k * LANES : (k + 2) * LANES] = dot3(left, split(pair))
    out_ref[:, wide : wide + 2 * LANES] = dot6(turned, panels)


def lower_inverse(tiles):
    count = len(tiles)
    tiles = list(tiles)
    lane = lax.broadcasted_iota(jnp.int32, (SUB, LANES), 1)
    row = lax.broadcasted_iota(jnp.int32, (SUB, LANES), 0)
    whole = lambda x: jnp.broadcast_to(x, (SUB, LANES))
    done = []
    for t in range(count):
        base = SUB * t
        here = tiles[t]
        inside = (lane >= base) & (lane < base + SUB)
        columns = [whole(here[:, base + v : base + v + 1]) for v in range(SUB)]
        d = {(u, v): whole(columns[v][u : u + 1, :]) for u in range(SUB) for v in range(u + 1)}
        l, r = {}, []
        for u in range(SUB):
            r.append(lax.rsqrt(d[u, u]))
            for v in range(u + 1, SUB):
                l[v, u] = d[v, u] * r[u]
            for v in range(u + 1, SUB):
                for w in range(v, SUB):
                    d[w, v] = d[w, v] - l[w, u] * l[v, u]
        start = jnp.where(inside, (lane - base == row).astype(F32), here)
        y = []
        for u in range(SUB):
            total = whole(start[u : u + 1, :])
            for w in range(u):
                total = total - l[u, w] * y[w]
            y.append(total * r[u])
        tile = y[0]
        for u in range(1, SUB):
            tile = jnp.where(row == u, y[u], tile)
        done.append(jnp.where(lane <= row + base, tile, 0.0))
        if t + 1 < count:
            v = [None] * SUB
            for u in reversed(range(SUB)):
                total = y[u]
                for w in range(u + 1, SUB):
                    total = total - l[w, u] * v[w]
                v[u] = total * r[u]
            for i in range(t + 1, count):
                total = jnp.where(inside, 0.0, tiles[i])
                for u in range(SUB):
                    total = total - whole(tiles[i][:, base + u : base + u + 1]) * v[u]
                tiles[i] = total
    return done


def final_kernel(scale, column, mine_ref, other_ref, m_ref, wg_ref, factors_ref, upper_ref, s_ref, x_ref):
    rows = mine_ref.shape[0]
    blocks = m_ref.shape[0] // rows
    wide = blocks * LANES
    place = column[0]
    n = LANES
    count = n // SUB

    s_ref[0] = wg_ref[0:n, wide : wide + n]
    s_ref[1] = wg_ref[n : 2 * n, wide + n : wide + 2 * n]
    cross = wg_ref[0:n, wide + n : wide + 2 * n]

    def turn(step, carry):
        tiles = lower_inverse([s_ref[step, SUB * t : SUB * (t + 1), :] for t in range(count)])
        for t in range(count):
            x_ref[step, SUB * t : SUB * (t + 1), :] = tiles[t]

        @pl.when(step == 0)
        def _():
            r12 = dot6(x_ref[0], cross)
            s_ref[1] = s_ref[1] - dot6(r12, r12, ((0,), (0,)))
            s_ref[0] = dot6(r12, x_ref[0], ((0,), (0,)))

        return carry

    lax.fori_loop(0, 2, turn, 0)
    x21 = -dot6(x_ref[1], s_ref[0])
    inverse = jnp.concatenate(
        [
            jnp.concatenate([x_ref[0], jnp.zeros((n, n), F32)], axis=1),
            jnp.concatenate([x21, x_ref[1]], axis=1),
        ],
        axis=0,
    )
    turned = inverse.T
    inverse_split, turned_split = split(inverse), split(turned)
    swapped = lax.rem(place, 2) == 1
    mine, other = mine_ref[...], other_ref[...]
    panels = split(
        jnp.concatenate([jnp.where(swapped, other, mine), jnp.where(swapped, mine, other)], axis=1)
    )
    owner = place < 2
    lead = jnp.where(place == 0, turned[:, 0:n], turned[:, n : 2 * n]) * (-scale)
    for k in range(0, blocks, 2):
        coef = dot3(inverse_split, split(wg_ref[:, k * n : (k + 2) * n]))
        for j in range(2):
            upper_ref[pl.ds(k + j, 2 * n, stride=blocks), :] = coef[:, j * n : (j + 1) * n] * (1.0 / scale)
        weights = dot3(turned_split, split(coef))
        left = m_ref[pl.ds(k, rows, stride=blocks), :]
        right = m_ref[pl.ds(k + 1, rows, stride=blocks), :]
        if k == 0:
            weights = jnp.concatenate([jnp.where(owner, lead, weights[:, 0:n]), weights[:, n : 2 * n]], axis=1)
            left = jnp.where(owner, 0.0, left)
        change = dot3(panels, split(weights))
        factors_ref[pl.ds(k, rows, stride=blocks), :] = left - change[:, 0:n]
        factors_ref[pl.ds(k + 1, rows, stride=blocks), :] = right - change[:, n : 2 * n]


VMEM_LIMIT = 56 * 2**20
IN_VMEM = pl.BlockSpec(memory_space=pltpu.VMEM)
IN_SMEM = pl.BlockSpec(memory_space=pltpu.SMEM)


def gram(core, mine, other, m2):
    rows = mine.shape[0]
    blocks = m2.shape[0] // rows
    return pl.pallas_call(
        gram_kernel,
        out_shape=jax.ShapeDtypeStruct((2 * LANES, (blocks + 2) * LANES), F32),
        in_specs=[IN_SMEM, IN_VMEM, IN_VMEM, IN_VMEM],
        out_specs=IN_VMEM,
        compiler_params=pltpu.CompilerParams(vmem_limit_bytes=VMEM_LIMIT),
        name="gram",
    )(core, mine, other, m2)


def finish(scale, column, mine, other, m2, wg):
    rows = mine.shape[0]
    blocks = m2.shape[0] // rows
    return pl.pallas_call(
        functools.partial(final_kernel, scale),
        out_shape=(
            jax.ShapeDtypeStruct(m2.shape, F32),
            jax.ShapeDtypeStruct((2 * LANES * blocks, LANES), F32),
        ),
        in_specs=[IN_SMEM, IN_VMEM, IN_VMEM, IN_VMEM, IN_VMEM],
        out_specs=(IN_VMEM, IN_VMEM),
        scratch_shapes=[pltpu.VMEM((2, LANES, LANES), F32), pltpu.VMEM((2, LANES, LANES), F32)],
        compiler_params=pltpu.CompilerParams(vmem_limit_bytes=VMEM_LIMIT),
        name="finish",
    )(column, mine, other, m2, wg)


def both_cores(pairs):
    return [(2 * a + c, 2 * b + c) for a, b in pairs for c in range(2)]


def spread_panels(lead):
    chip = lax.axis_index("col") // 2
    send = lambda x, pairs: lax.ppermute(x, "col", both_cores(pairs))
    far = send(lead, [(0, 3)]), send(lead, [(0, 5)])
    held = jnp.where(chip == 0, lead, 0.0) + far[0] + far[1]
    near = send(held, [(0, 1), (3, 4), (5, 6)]), send(held, [(0, 7), (3, 2)])
    mine = held + near[0] + near[1]
    other = lax.ppermute(mine, "col", [(i, i ^ 1) for i in range(16)])
    return mine, other


def total_over_rows(part):
    size = lax.axis_size("row")
    height, width = part.shape
    piece = height // size
    got = lax.all_to_all(part, "row", 0, 0, tiled=True)
    mine = jnp.sum(got.reshape(size, piece, width), axis=0)
    repeated = jnp.broadcast_to(mine[None], (size, piece, width)).reshape(height, width)
    return lax.all_to_all(repeated, "row", 0, 0, tiled=True)


def shards(matrix):
    rows, blocks, lanes = matrix.shape
    scale = math.sqrt(rows * lax.axis_size("row"))
    m2 = matrix.reshape(rows * blocks, lanes)
    column = lax.axis_index("col").astype(jnp.int32).reshape(1)
    mine, other = spread_panels(matrix[:, 0, :])
    wg = total_over_rows(gram(lax.rem(column, 2), mine, other, m2))
    factors, upper = finish(scale, column, mine, other, m2, wg)
    return factors.reshape(matrix.shape), upper.reshape(2 * LANES, blocks, lanes)


def solution(mesh):
    in_specs = (P("row", None, "col"),)
    out_specs = (P("row", None, "col"), P(None, None, "col"))
    return jax.shard_map(shards, mesh=mesh, in_specs=in_specs, out_specs=out_specs, check_vma=False)
```

time: 2090 us -> 127 us (0.06); the launches traced: 2060 us -> 125 us
  other arithmetic: 1200 us -> 0.25 us
  waiting for transfers between devices: 595 us -> 29.3 us
  loops' own time: 192 us -> 0 us
  blocking collectives: 0 us -> 49.2 us
  matrix products: 43 us -> 0 us
  Pallas kernels: 0 us -> 29.3 us
    reduce_sum x1280 -> x1, other arithmetic: 602 us -> 0.07 us  [total_over_rows(): mine = jnp.sum(got.reshape(size, piece, width), axis=0)]
    psum x6 -> x0, waiting for transfers between devices: 595 us -> none  [the longest x2 220 us: spread(): return lax.psum(jnp.where(mine, array, jnp.zeros_like(array)), axis)]
    add x512 -> x2, other arithmetic: 419 us -> 0.19 us  [the longest x1 0.1 us: spread_panels(): mine = held + near[0] + near[1]]
    another operation x4 -> x0, loops' own time: 192 us -> none  [the longest x2 181 us: upper_factor(): rest, lower = lax.fori_loop(0, size, turn, (gram, jnp.zeros_like(gram)))]
    div x257 -> x0, other arithmetic: 168 us -> none  [the longest x256 168 us: turn(): new_row = (unit - jnp.sum(row_vals[:, None] * inverse, axis=0)) / pivot]
    all_to_all x0 -> x2, blocking collectives: none -> 49.2 us  [the longest x1 26.4 us: total_over_rows(): got = lax.all_to_all(part, 'row', 0, 0, tiled=True)]
    dot_general x8 -> x0, matrix products: 43 us -> none  [the longest x2 17.9 us: project(): jnp.einsum('rp,rbc->pbc', basis, work, precision=lax.Precision.HIGHEST, p...]
    ppermute x0 -> x5, waiting for transfers between devices: none -> 29.3 us  [the longest x4 27.3 us: spread_panels(): send = lambda x, pairs: lax.ppermute(x, 'col', both_cores(pairs))]
  transfers between devices with their start and end apart: 6 -> 5, of which waited for: 6 -> 5; matrix products, arithmetic and copies ran while one was open for 0% -> 0% of each run, Pallas kernels for 0% -> 0%
where the time goes in v1:
time: 127 us; the launch traced here: 125 us
  blocking collectives  49.2 us (39%)
  waiting for transfers between devices  29.3 us (23%)
  Pallas kernels  29.3 us (23%)
  starting transfers between devices  12.8 us (10%)
  local copies, waits for them, and re-layouts  3.68 us (3%)
    ppermute x4, waiting for transfers between devices, spread_panels(): send = lambda x, pairs: lax.ppermute(x, 'col', both_cores(pairs))  27.3 us
    all_to_all x1, blocking collectives, total_over_rows(): got = lax.all_to_all(part, 'row', 0, 0, tiled=True)  26.4 us
    all_to_all x1, blocking collectives, total_over_rows(): return lax.all_to_all(repeated, 'row', 0, 0, tiled=True)  22.8 us
    pallas_call x1, Pallas kernels, finish(): pl.pallas_call(functools.partial(final_kernel, scale), out_shape=(jax.Sha...  21.4 us
    ppermute x4, starting transfers between devices, spread_panels(): send = lambda x, pairs: lax.ppermute(x, 'col', both_cores(pairs))  12.7 us
    pallas_call x1, Pallas kernels, gram(): pl.pallas_call(gram_kernel, out_shape=jax.ShapeDtypeStruct((2 * LANES, (b...  7.89 us
    slice x1, local copies, waits for them, and re-layouts, shards(): mine, other = spread_panels(matrix[:, 0, :])  2.73 us
  transfers between devices with their start and end apart: 5, of which 5 were waited for; matrix products, arithmetic and copies ran while one was open for 0% of the time, Pallas kernels for 0%

profile of v1, /device:TPU:2, one launch (start us, length us, event | category | flops | bytes accessed | tf_op | source)
XLA Modules:
  0.0 125.3 jit_solution(17656895141222750209)
XLA Ops:
  0.6 2.7 %slice.3 = f32[1280,1,128]{2,1,0:T(1,128)S(1)} slice(f32[1280,8,128]{2,1,0:T(8,128)} %param.1), slice={[0:1280], [0:1], [0:128]} | slice | bytes 1310720 | tf_op jit(solution)/shard_map/slice | solution.py:222
  3.4 8.7 %collective-permute-start.1 = (f32[1280,128]{1,0:T(8,128)S(1)}, f32[1280,128]{1,0:T(8,128)S(1)}, u32[]{:S(2)}, u32[]{:S(2)}) collective-permute-start(f32[1280,128]{1,0:T(8,128)S(1)} %bitcast.13), channel_id=1, source_target_pairs={{0,10},{1,11},{16,26},{17,27},{32,42},{33,43},{48,58},{49,59},{64,... | collective-permute-start | bytes 1966088 | tf_op jit(solution)/shard_map/ppermute | solution.py:198
  12.1 1.3 %collective-permute-start = (f32[1280,128]{1,0:T(8,128)S(1)}, f32[1280,128]{1,0:T(8,128)S(1)}, u32[]{:S(2)}, u32[]{:S(2)}) collective-permute-start(f32[1280,128]{1,0:T(8,128)S(1)} %bitcast.14), channel_id=1, source_target_pairs={{0,6},{1,7},{16,22},{17,23},{32,38},{33,39},{48,54},{49,55},{64,70... | collective-permute-start | bytes 1966088 | tf_op jit(solution)/shard_map/ppermute | solution.py:198
  13.4 12.6 %collective-permute-done.1 = f32[1280,128]{1,0:T(8,128)S(1)} collective-permute-done((f32[1280,128]{1,0:T(8,128)S(1)}, f32[1280,128]{1,0:T(8,128)S(1)}, u32[]{:S(2)}, u32[]{:S(2)}) %collective-permute-start.1) | collective-permute-done | bytes 655392 | tf_op jit(solution)/shard_map/ppermute | solution.py:198
  26.0 1.3 %collective-permute-done = f32[1280,128]{1,0:T(8,128)S(1)} collective-permute-done((f32[1280,128]{1,0:T(8,128)S(1)}, f32[1280,128]{1,0:T(8,128)S(1)}, u32[]{:S(2)}, u32[]{:S(2)}) %collective-permute-start) | collective-permute-done | bytes 655392 | tf_op jit(solution)/shard_map/ppermute | solution.py:198
  27.3 0.1 add_add_fusion.1
  27.4 1.3 %collective-permute-start.3 = (f32[1280,128]{1,0:T(8,128)S(1)}, f32[1280,128]{1,0:T(8,128)S(1)}, u32[]{:S(2)}, u32[]{:S(2)}) collective-permute-start(f32[1280,128]{1,0:T(8,128)S(1)} %add_add_fusion.1), channel_id=1, source_target_pairs={{0,14},{1,15},{6,4},{7,5},{16,30},{17,31},{22,20},{23,21},{32,46},... | collective-permute-start | bytes 1966088 | tf_op jit(solution)/shard_map/ppermute | solution.py:198
  28.8 1.3 %collective-permute-start.2 = (f32[1280,128]{1,0:T(8,128)S(1)}, f32[1280,128]{1,0:T(8,128)S(1)}, u32[]{:S(2)}, u32[]{:S(2)}) collective-permute-start(f32[1280,128]{1,0:T(8,128)S(1)} %add_add_fusion.1), channel_id=1, source_target_pairs={{0,2},{1,3},{6,8},{7,9},{10,12},{11,13},{16,18},{17,19},{22,24},{2... | collective-permute-start | bytes 1966088 | tf_op jit(solution)/shard_map/ppermute | solution.py:198
  30.1 12.0 %collective-permute-done.3 = f32[1280,128]{1,0:T(8,128)S(1)} collective-permute-done((f32[1280,128]{1,0:T(8,128)S(1)}, f32[1280,128]{1,0:T(8,128)S(1)}, u32[]{:S(2)}, u32[]{:S(2)}) %collective-permute-start.3) | collective-permute-done | bytes 655392 | tf_op jit(solution)/shard_map/ppermute | solution.py:198
  42.1 1.3 %collective-permute-done.2 = f32[1280,128]{1,0:T(8,128)S(1)} collective-permute-done((f32[1280,128]{1,0:T(8,128)S(1)}, f32[1280,128]{1,0:T(8,128)S(1)}, u32[]{:S(2)}, u32[]{:S(2)}) %collective-permute-start.2) | collective-permute-done | bytes 655392 | tf_op jit(solution)/shard_map/ppermute | solution.py:198
  43.4 0.1 add_add_fusion.mine_ref
  43.5 0.0 copy-start
  43.6 0.1 collective-permute-start.4
  43.7 2.1 %collective-permute-done.4.other_ref = f32[1280,128]{1,0:T(8,128)S(1)} collective-permute-done((f32[1280,128]{1,0:T(8,128)S(1)}, f32[1280,128]{1,0:T(8,128)S(1)}, u32[]{:S(2)}, u32[]{:S(2)}) %collective-permute-start.4) | collective-permute-done | bytes 655392 | tf_op jit(solution)/shard_map/ppermute | solution.py:203
  45.7 0.0 copy-start.1
  45.7 0.0 copy-done
  45.7 0.8 copy-done.1
  46.6 7.9 %gram.1 = f32[256,1280]{1,0:T(8,128)} custom-call(s32[1]{0:T(128)S(6)} %rem.38.second_core, f32[1280,128]{1,0:T(8,128)} %copy-done, f32[1280,128]{1,0:T(8,128)} %copy-done.1, f32[10240,128]{1,0:T(8,128)} %bitcast.9), custom_call_target="tpu_custom_call" | custom-call | tf_op jit(solution)/shard_map/gram/pallas_call | solution.py:165
  54.5 26.4 %all_to_all.17 = f32[16,16,1280]{2,1,0:T(8,128)S(1)} all-to-all(f32[16,16,1280]{2,1,0:T(8,128)} %bitcast.12), channel_id=1, replica_groups=mesh['row'=16,'col'=16] {'row'}, dimensions={0} | all-to-all | bytes 2621440 | tf_op jit(solution)/shard_map/all_to_all | solution.py:211
  80.8 0.1 reduce_sum.9
  80.9 0.1 broadcast_in_dim.11
  81.0 22.8 %all_to_all.18 = f32[16,16,1280]{2,1,0:T(8,128)} all-to-all(f32[16,16,1280]{2,1,0:T(8,128)S(1)} %broadcast_in_dim.11), channel_id=1, replica_groups=mesh['row'=16,'col'=16] {'row'}, dimensions={0} | all-to-all | bytes 2621440 | tf_op jit(solution)/shard_map/all_to_all | solution.py:214
  103.9 21.4 %finish.1 = (f32[10240,128]{1,0:T(8,128)}, f32[2048,128]{1,0:T(8,128)}) custom-call(s32[1]{0:T(128)} %bitcast.column, f32[1280,128]{1,0:T(8,128)} %copy-done, f32[1280,128]{1,0:T(8,128)} %copy-done.1, f32[10240,128]{1,0:T(8,128)} %bitcast.10, f32[256,1280]{1,0:T(8,128)} %bitcast.11), custom_call_target="tpu_custom_call" | custom-call | tf_op jit(solution)/shard_map/finish/pallas_call | solution.py:178
Async XLA Ops:
  3.4 22.6 %collective-permute-start.1 = (f32[1280,128]{1,0:T(8,128)S(1)}, f32[1280,128]{1,0:T(8,128)S(1)}, u32[]{:S(2)}, u32[]{:S(2)}) collective-permute-start(f32[1280,128]{1,0:T(8,128)S(1)} %bitcast.13), channel_id=1, source_target_pairs={{0,10},{1,11},{16,26},{17,27},{32,42},{33,43},{48,58},{49,59},{64,... | collective-permute-start | bytes 1966088 | tf_op jit(solution)/shard_map/ppermute | solution.py:198
  12.1 15.3 %collective-permute-start = (f32[1280,128]{1,0:T(8,128)S(1)}, f32[1280,128]{1,0:T(8,128)S(1)}, u32[]{:S(2)}, u32[]{:S(2)}) collective-permute-start(f32[1280,128]{1,0:T(8,128)S(1)} %bitcast.14), channel_id=1, source_target_pairs={{0,6},{1,7},{16,22},{17,23},{32,38},{33,39},{48,54},{49,55},{64,70... | collective-permute-start | bytes 1966088 | tf_op jit(solution)/shard_map/ppermute | solution.py:198
  27.4 14.7 %collective-permute-start.3 = (f32[1280,128]{1,0:T(8,128)S(1)}, f32[1280,128]{1,0:T(8,128)S(1)}, u32[]{:S(2)}, u32[]{:S(2)}) collective-permute-start(f32[1280,128]{1,0:T(8,128)S(1)} %add_add_fusion.1), channel_id=1, source_target_pairs={{0,14},{1,15},{6,4},{7,5},{16,30},{17,31},{22,20},{23,21},{32,46},... | collective-permute-start | bytes 1966088 | tf_op jit(solution)/shard_map/ppermute | solution.py:198
  28.8 14.7 %collective-permute-start.2 = (f32[1280,128]{1,0:T(8,128)S(1)}, f32[1280,128]{1,0:T(8,128)S(1)}, u32[]{:S(2)}, u32[]{:S(2)}) collective-permute-start(f32[1280,128]{1,0:T(8,128)S(1)} %add_add_fusion.1), channel_id=1, source_target_pairs={{0,2},{1,3},{6,8},{7,9},{10,12},{11,13},{16,18},{17,19},{22,24},{2... | collective-permute-start | bytes 1966088 | tf_op jit(solution)/shard_map/ppermute | solution.py:198
  43.5 2.2 %copy-start = (f32[1280,128]{1,0:T(8,128)}, f32[1280,128]{1,0:T(8,128)S(1)}, u32[]{:S(2)}) copy-start(f32[1280,128]{1,0:T(8,128)S(1)} %add_add_fusion.mine_ref) | copy-start | bytes 1966084
  43.6 2.2 %collective-permute-start.4 = (f32[1280,128]{1,0:T(8,128)S(1)}, f32[1280,128]{1,0:T(8,128)S(1)}, u32[]{:S(2)}, u32[]{:S(2)}) collective-permute-start(f32[1280,128]{1,0:T(8,128)S(1)} %add_add_fusion.mine_ref), channel_id=1, source_target_pairs={{0,1},{1,0},{2,3},{3,2},{4,5},{5,4},{6,7},{7,6},{8,9},{9,8},{10,11... | collective-permute-start | bytes 1966088 | tf_op jit(solution)/shard_map/ppermute | solution.py:203
  45.7 0.8 copy-start.1

commit v2 on v1

v2 whole, which is shorter than its diff:
```python
import functools
import math

import jax
import jax.numpy as jnp
from jax import lax
from jax.experimental import pallas as pl
from jax.experimental.pallas import tpu as pltpu
from jax.sharding import PartitionSpec as P

F32 = jnp.float32
BF16 = jnp.bfloat16
HIGHEST = lax.Precision.HIGHEST
LANES = 128
SUB = 8
RANKS = 16
BUDGET = dict(gram=16, halves=50, wide=32, total=16, factor=16, basis=24, finish=54)


def split(x):
    high = x.astype(BF16)
    low = (x - high.astype(F32)).astype(BF16)
    return high, low


def dot3(a, b):
    left = jnp.concatenate([a[0], a[0], a[1]], axis=1)
    right = jnp.concatenate([b[0], b[1], b[0]], axis=0)
    return jnp.dot(left, right, preferred_element_type=F32)


def dot6(a, b, dims=((1,), (0,))):
    return lax.dot_general(a, b, (dims, ((), ())), precision=HIGHEST, preferred_element_type=F32)


def panels_of(second_core, mine_ref, other_ref):
    mine, other = mine_ref[...], other_ref[...]
    return jnp.concatenate(
        [jnp.where(second_core, other, mine), jnp.where(second_core, mine, other)], axis=1
    )


def gram_kernel(column, mine_ref, other_ref, out_ref):
    panels = panels_of(lax.rem(column[0], 2) == 1, mine_ref, other_ref)
    out_ref[...] = dot6(panels.T, panels)


def halves_kernel(column, m_ref, high_ref, low_ref):
    blocks = m_ref.shape[0] // high_ref.shape[0]
    for k in range(blocks):
        here = slice(k * LANES, (k + 1) * LANES)
        high_ref[:, here], low_ref[:, here] = split(m_ref[pl.ds(k, high_ref.shape[0], stride=blocks), :])


def wide_kernel(column, mine_ref, other_ref, high_ref, low_ref, out_ref):
    left = split(panels_of(lax.rem(column[0], 2) == 1, mine_ref, other_ref).T)
    step = 2 * LANES
    for k in range(0, out_ref.shape[1], step):
        here = slice(k, k + step)
        out_ref[:, here] = dot3(left, (high_ref[:, here], low_ref[:, here]))


def total_kernel(column, part_ref, out_ref):
    piece = part_ref.shape[0] // RANKS
    total = part_ref[0:piece, :]
    for r in range(1, RANKS):
        total = total + part_ref[r * piece : (r + 1) * piece, :]
    for r in range(RANKS):
        out_ref[r * piece : (r + 1) * piece, :] = total


def lower_inverse(tiles):
    count = len(tiles)
    tiles = list(tiles)
    lane = lax.broadcasted_iota(jnp.int32, (SUB, LANES), 1)
    row = lax.broadcasted_iota(jnp.int32, (SUB, LANES), 0)
    whole = lambda x: jnp.broadcast_to(x, (SUB, LANES))
    done = []
    for t in range(count):
        base = SUB * t
        here = tiles[t]
        inside = (lane >= base) & (lane < base + SUB)
        columns = [whole(here[:, base + v : base + v + 1]) for v in range(SUB)]
        d = {(u, v): whole(columns[v][u : u + 1, :]) for u in range(SUB) for v in range(u + 1)}
        l, r = {}, []
        for u in range(SUB):
            r.append(lax.rsqrt(d[u, u]))
            for v in range(u + 1, SUB):
                l[v, u] = d[v, u] * r[u]
            for v in range(u + 1, SUB):
                for w in range(v, SUB):
                    d[w, v] = d[w, v] - l[w, u] * l[v, u]
        start = jnp.where(inside, (lane - base == row).astype(F32), here)
        y = []
        for u in range(SUB):
            total = whole(start[u : u + 1, :])
            for w in range(u):
                total = total - l[u, w] * y[w]
            y.append(total * r[u])
        tile = y[0]
        for u in range(1, SUB):
            tile = jnp.where(row == u, y[u], tile)
        done.append(jnp.where(lane <= row + base, tile, 0.0))
        if t + 1 < count:
            v = [None] * SUB
            for u in reversed(range(SUB)):
                total = y[u]
                for w in range(u + 1, SUB):
                    total = total - l[w, u] * v[w]
                v[u] = total * r[u]
            for i in range(t + 1, count):
                total = jnp.where(inside, 0.0, tiles[i])
                for u in range(SUB):
                    total = total - whole(tiles[i][:, base + u : base + u + 1]) * v[u]
                tiles[i] = total
    return done


def factor_kernel(column, g_ref, x_ref, s_ref):
    n = LANES
    count = n // SUB
    s_ref[0] = g_ref[0:n, 0:n]
    s_ref[1] = g_ref[n : 2 * n, n : 2 * n]

    def turn(step, carry):
        tiles = lower_inverse([s_ref[step, SUB * t : SUB * (t + 1), :] for t in range(count)])
        for t in range(count):
            x_ref[step, SUB * t : SUB * (t + 1), :] = tiles[t]

        @pl.when(step == 0)
        def _():
            r12 = dot6(x_ref[0], g_ref[0:n, n : 2 * n])
            s_ref[1] = s_ref[1] - dot6(r12, r12, ((0,), (0,)))
            s_ref[0] = dot6(r12, x_ref[0], ((0,), (0,)))

        return carry

    lax.fori_loop(0, 2, turn, 0)
    x_ref[2] = -dot6(x_ref[1], s_ref[0])


def whole_inverse(x_ref):
    n = LANES
    return jnp.concatenate(
        [
            jnp.concatenate([x_ref[0], jnp.zeros((n, n), F32)], axis=1),
            jnp.concatenate([x_ref[2], x_ref[1]], axis=1),
        ],
        axis=0,
    )


def basis_kernel(column, mine_ref, other_ref, x_ref, high_ref, low_ref):
    panels = panels_of(lax.rem(column[0], 2) == 1, mine_ref, other_ref)
    high_ref[...], low_ref[...] = split(dot3(split(panels), split(whole_inverse(x_ref).T)))


def final_kernel(
    scale, column, high_ref, low_ref, m_ref, w_ref, x_ref, factors_ref, upper_ref, coef_ref, ch_ref, cl_ref
):
    rows = high_ref.shape[0]
    blocks = m_ref.shape[0] // rows
    place = column[0]
    n = LANES
    owner = place < 2
    turn = pl.program_id(0)

    @pl.when(turn == 0)
    def _():
        inverse = split(whole_inverse(x_ref))
        unit = lax.broadcasted_iota(jnp.int32, (2 * n, n), 0) == lax.broadcasted_iota(jnp.int32, (2 * n, n), 1) + place * n
        unit = jnp.where(unit, -scale, 0.0)
        for k in range(0, blocks, 2):
            here = slice(k * n, (k + 2) * n)
            coef = dot3(inverse, split(w_ref[:, here]))
            coef_ref[:, here] = coef * (1.0 / scale)
            if k == 0:
                coef = jnp.concatenate([jnp.where(owner, unit, coef[:, 0:n]), coef[:, n : 2 * n]], axis=1)
            ch_ref[:, here], cl_ref[:, here] = split(coef)

    basis = high_ref[...], low_ref[...]
    for k in range(0, blocks, 2):
        here = slice(k * n, (k + 2) * n)
        change = dot3(basis, (ch_ref[:, here], cl_ref[:, here]))
        left = m_ref[pl.ds(k, rows, stride=blocks), :]
        if k == 0:
            left = jnp.where(owner, 0.0, left)
        factors_ref[pl.ds(k, rows, stride=blocks), :] = left - change[:, 0:n]
        factors_ref[pl.ds(k + 1, rows, stride=blocks), :] = (
            m_ref[pl.ds(k + 1, rows, stride=blocks), :] - change[:, n : 2 * n]
        )
    some = upper_ref.shape[0] // blocks
    for k in range(blocks):
        upper_ref[pl.ds(k, some, stride=blocks), :] = coef_ref[
            pl.ds(pl.multiple_of(turn * some, some), some), k * n : (k + 1) * n
        ]


IN_SMEM = pl.BlockSpec(memory_space=pltpu.SMEM)


def by_rows(array, steps):
    return pl.BlockSpec((array.shape[0] // steps, array.shape[1]), lambda i: (i, 0))


def fixed(array):
    return pl.BlockSpec(array.shape, lambda i: (0,) * len(array.shape))


def kernel_call(body, name, micros, steps, operands, out_shape, row_split, scratch=()):
    specs = [by_rows(x, steps) if s else fixed(x) for x, s in zip((*operands[1:], *out_shape), row_split)]
    return pl.pallas_call(
        body,
        grid=(steps,),
        out_shape=out_shape,
        in_specs=[IN_SMEM] + specs[: len(operands) - 1],
        out_specs=tuple(specs[len(operands) - 1 :]),
        scratch_shapes=list(scratch),
        compiler_params=pltpu.CompilerParams(vmem_limit_bytes=BUDGET[name] * 2**20),
        cost_estimate=pl.CostEstimate(flops=micros * 10**9, bytes_accessed=micros * 10**6, transcendentals=0),
        name=name,
    )(*operands)


def shape(*dims):
    return jax.ShapeDtypeStruct(dims, F32)


def both_cores(pairs):
    return [(2 * a + c, 2 * b + c) for a, b in pairs for c in range(2)]


def send(x, pairs):
    return lax.ppermute(x, "col", both_cores(pairs))


def spread_far(x, chip):
    far = send(x, [(0, 3)]), send(x, [(0, 5)])
    return jnp.where(chip == 0, x, 0.0) + far[0] + far[1]


def spread_near(x):
    return send(x, [(0, 1), (3, 4), (5, 6)]), send(x, [(0, 7), (3, 2)])


def total(column, part):
    return kernel_call(total_kernel, "total", 1, 1, (column, part), (shape(*part.shape),), (0, 0))[0]


def exchange(x):
    return lax.all_to_all(x, "row", 0, 0, tiled=True)


def shards(matrix):
    rows, blocks, lanes = matrix.shape
    size = lax.axis_size("row")
    scale = math.sqrt(rows * size)
    steps = 4
    m2 = matrix.reshape(rows * blocks, lanes)
    column = lax.axis_index("col").astype(jnp.int32).reshape(1)
    chip = lax.axis_index("col") // 2
    lead = matrix[:, 0, :]
    n = 2 * lanes
    partner = lax.ppermute(lead, "col", [(0, 1), (1, 0)])
    (part,) = kernel_call(gram_kernel, "gram", 3, 1, (column, lead, partner), (shape(n, n),), (0, 0, 0))
    half = jax.ShapeDtypeStruct((rows, blocks * lanes), BF16)
    later, part = lax.optimization_barrier((column, part))
    m_high, m_low = kernel_call(halves_kernel, "halves", 4, steps, (later, m2), (half, half), (1, 1, 1))
    part = exchange(part)
    far = send(lead, [(0, 3)]), send(lead, [(0, 5)])
    far, _, _ = lax.optimization_barrier((far, m_high, m_low))
    held = jnp.where(chip == 0, lead, 0.0) + far[0] + far[1]
    part, held = lax.optimization_barrier((part, held))
    near = spread_near(held)
    gram = exchange(total(column, part))
    near, gram = lax.optimization_barrier((near, gram))
    mine = held + near[0] + near[1]
    other = lax.ppermute(mine, "col", [(i, i ^ 1) for i in range(16)])
    (wide,) = kernel_call(
        wide_kernel, "wide", 6, 1, (column, mine, other, m_high, m_low), (shape(n, blocks * lanes),), (0,) * 5
    )
    gram, wide = lax.optimization_barrier((gram, wide))
    wide = exchange(wide)
    (factor,) = kernel_call(
        factor_kernel, "factor", 12, 1, (column, gram), (shape(3, lanes, lanes),), (0, 0),
        scratch=[pltpu.VMEM((2, lanes, lanes), F32)],
    )
    _, wide = lax.optimization_barrier((factor, wide))
    factor_far = spread_far(factor, chip)
    wide = exchange(total(column, wide))
    near = spread_near(factor_far)
    factor = factor_far + near[0] + near[1]
    half = jax.ShapeDtypeStruct((rows, n), BF16)
    high, low = kernel_call(
        basis_kernel, "basis", 2, 1, (column, mine, other, factor), (half, half), (0, 0, 0, 0, 0)
    )
    factors, upper = kernel_call(
        functools.partial(final_kernel, scale), "finish", 6, steps,
        (column, high, low, m2, wide, factor), (shape(*m2.shape), shape(n * blocks, lanes)),
        (1, 1, 1, 0, 0, 1, 1), scratch=[pltpu.VMEM((n, blocks * lanes), t) for t in (F32, BF16, BF16)],
    )
    return factors.reshape(matrix.shape), upper.reshape(n, blocks, lanes)


def solution(mesh):
    in_specs = (P("row", None, "col"),)
    out_specs = (P("row", None, "col"), P(None, None, "col"))
    return jax.shard_map(shards, mesh=mesh, in_specs=in_specs, out_specs=out_specs, check_vma=False)
```

time: 127 us -> 109 us (0.86)
  blocking collectives: 49.2 us -> 13.8 us
  starting transfers between devices: 12.8 us -> 43.7 us
  waiting for transfers between devices: 29.3 us -> 11.3 us
  Pallas kernels: 29.3 us -> 32.3 us
  local copies, waits for them, and re-layouts: 3.68 us -> 5.95 us
    all_to_all x2 -> x1, blocking collectives: 49.2 us -> 13.8 us  [exchange(): return lax.all_to_all(x, 'row', 0, 0, tiled=True)]
    ppermute x5 -> x10, waiting for transfers between devices: 29.3 us -> 5.26 us  [the longest x8 3.17 us: send(): return lax.ppermute(x, 'col', both_cores(pairs))]
    all_to_all x0 -> x3, starting transfers between devices: none -> 20.9 us  [exchange(): return lax.all_to_all(x, 'row', 0, 0, tiled=True)]
    ppermute x5 -> x10, starting transfers between devices: 12.8 us -> 22.8 us  [the longest x8 20.8 us: send(): return lax.ppermute(x, 'col', both_cores(pairs))]
    all_to_all x0 -> x3, waiting for transfers between devices: none -> 6 us  [exchange(): return lax.all_to_all(x, 'row', 0, 0, tiled=True)]
    pallas_call x2 -> x8, Pallas kernels: 29.3 us -> 32.3 us  [kernel_call(): pl.pallas_call(body, grid=(steps,), out_shape=out_shape, in_specs=[IN_SME...]
    unnamed x4 -> x12, local copies, waits for them, and re-layouts: 0.83 us -> 3.23 us
  transfers between devices with their start and end apart: 5 -> 13, of which waited for: 5 -> 5; matrix products, arithmetic and copies ran while one was open for 0% -> 0% of each run, Pallas kernels for 0% -> 19%
where the time goes in v2:
time: 109 us; the launch traced here: 108 us
  starting transfers between devices  43.7 us (40%)
  Pallas kernels  32.3 us (30%)
  blocking collectives  13.8 us (13%)
  waiting for transfers between devices  11.3 us (10%)
  local copies, waits for them, and re-layouts  5.95 us (5%)
    pallas_call x8, Pallas kernels, kernel_call(): pl.pallas_call(body, grid=(steps,), out_shape=out_shape, in_specs=[IN_SME...  32.3 us
    all_to_all x3, starting transfers between devices, exchange(): return lax.all_to_all(x, 'row', 0, 0, tiled=True)  20.9 us
    ppermute x8, starting transfers between devices, send(): return lax.ppermute(x, 'col', both_cores(pairs))  20.8 us
    all_to_all x1, blocking collectives, exchange(): return lax.all_to_all(x, 'row', 0, 0, tiled=True)  13.8 us
    all_to_all x3, waiting for transfers between devices, exchange(): return lax.all_to_all(x, 'row', 0, 0, tiled=True)  6 us
    unnamed x12, local copies, waits for them, and re-layouts  3.23 us
    ppermute x8, waiting for transfers between devices, send(): return lax.ppermute(x, 'col', both_cores(pairs))  3.17 us
    slice x1, local copies, waits for them, and re-layouts, shards(): lead = matrix[:, 0, :]  2.73 us
  transfers between devices with their start and end apart: 13, of which 5 were waited for; matrix products, arithmetic and copies ran while one was open for 0% of the time, Pallas kernels for 19%

profile of v2, /device:TPU:2, one launch (start us, length us, event | category | flops | bytes accessed | tf_op | source)
XLA Modules:
  0.0 108.0 jit_solution(16430802089119149651)
XLA Ops:
  0.6 2.7 %slice.3 = f32[1280,1,128]{2,1,0:T(1,128)S(1)} slice(f32[1280,8,128]{2,1,0:T(8,128)} %param.1), slice={[0:1280], [0:1], [0:128]} | slice | bytes 1310720 | tf_op jit(solution)/shard_map/slice | solution.py:262
  3.4 1.9 %collective-permute-start = (f32[1280,128]{1,0:T(8,128)S(1)}, f32[1280,128]{1,0:T(8,128)S(1)}, u32[]{:S(2)}, u32[]{:S(2)}) collective-permute-start(f32[1280,128]{1,0:T(8,128)S(1)} %bitcast.15), channel_id=1, source_target_pairs={{0,1},{1,0},{16,17},{17,16},{32,33},{33,32},{48,49},{49,48},{64,65... | collective-permute-start | bytes 1966088 | tf_op jit(solution)/shard_map/ppermute | solution.py:264
  5.3 7.5 %collective-permute-start.2 = (f32[1280,128]{1,0:T(8,128)S(1)}, f32[1280,128]{1,0:T(8,128)S(1)}, u32[]{:S(2)}, u32[]{:S(2)}) collective-permute-start(f32[1280,128]{1,0:T(8,128)S(1)} %bitcast.16), channel_id=1, source_target_pairs={{0,10},{1,11},{16,26},{17,27},{32,42},{33,43},{48,58},{49,59},{64,... | collective-permute-start | bytes 1966088 | tf_op jit(solution)/shard_map/ppermute | solution.py:234
  12.8 1.3 %collective-permute-start.1 = (f32[1280,128]{1,0:T(8,128)S(1)}, f32[1280,128]{1,0:T(8,128)S(1)}, u32[]{:S(2)}, u32[]{:S(2)}) collective-permute-start(f32[1280,128]{1,0:T(8,128)S(1)} %bitcast.17), channel_id=1, source_target_pairs={{0,6},{1,7},{16,22},{17,23},{32,38},{33,39},{48,54},{49,55},{64,70... | collective-permute-start | bytes 1966088 | tf_op jit(solution)/shard_map/ppermute | solution.py:234
  14.1 2.1 %gram.1 = f32[256,256]{1,0:T(8,128)} custom-call(s32[1]{0:T(128)} %bitcast.column, f32[1280,128]{1,0:T(8,128)S(1)} %bitcast.18, f32[1280,128]{1,0:T(8,128)S(1)} %collective-permute-done.other_ref), custom_call_target="tpu_custom_call" | custom-call | flops 3000000000 | bytes 3000000 | tf_op jit(solution)/shard_map/gram/pallas_call | solution.py:212
  16.2 7.5 %all-to-all-start = ((f32[16,16,256]{2,1,0:T(8,128)}), f32[16,16,256]{2,1,0:T(8,128)S(1)}, u32[]{:S(2)}, u32[]{:S(2)}) async-start(f32[16,16,256]{2,1,0:T(8,128)} %bitcast.2), calls=%async_computation | async-start | bytes 524288 | tf_op jit(solution)/shard_map/all_to_all | solution.py:251
  23.7 5.1 %halves.1 = (bf16[1280,1024]{1,0:T(8,128)(2,1)S(1)}, bf16[1280,1024]{1,0:T(8,128)(2,1)}) custom-call(s32[1]{0:T(128)} %bitcast.column, f32[10240,128]{1,0:T(8,128)} %bitcast.24), custom_call_target="tpu_custom_call" | custom-call | flops 4000000000 | bytes 4000000 | tf_op jit(solution)/shard_map/halves/pallas_call | solution.py:212
  28.8 1.5 %copy-done.1 = bf16[1280,1024]{1,0:T(8,128)(2,1)} copy-done((bf16[1280,1024]{1,0:T(8,128)(2,1)}, bf16[1280,1024]{1,0:T(8,128)(2,1)S(1)}, u32[]{:S(2)}) %copy-start.1) | copy-done | bytes 2621464
  31.0 1.6 %collective-permute-start.4 = (f32[1280,128]{1,0:T(8,128)S(1)}, f32[1280,128]{1,0:T(8,128)S(1)}, u32[]{:S(2)}, u32[]{:S(2)}) collective-permute-start(f32[1280,128]{1,0:T(8,128)S(1)} %add_add_fusion.1), channel_id=1, source_target_pairs={{0,14},{1,15},{6,4},{7,5},{16,30},{17,31},{22,20},{23,21},{32,46},... | collective-permute-start | bytes 1966088 | tf_op jit(solution)/shard_map/ppermute | solution.py:234
  32.6 1.3 %collective-permute-start.3 = (f32[1280,128]{1,0:T(8,128)S(1)}, f32[1280,128]{1,0:T(8,128)S(1)}, u32[]{:S(2)}, u32[]{:S(2)}) collective-permute-start(f32[1280,128]{1,0:T(8,128)S(1)} %add_add_fusion.1), channel_id=1, source_target_pairs={{0,2},{1,3},{6,8},{7,9},{10,12},{11,13},{16,18},{17,19},{22,24},{2... | collective-permute-start | bytes 1966088 | tf_op jit(solution)/shard_map/ppermute | solution.py:234
  34.0 13.8 %all_to_all.47 = f32[16,16,256]{2,1,0:T(8,128)S(1)} all-to-all(f32[16,16,256]{2,1,0:T(8,128)S(1)} %bitcast.23), channel_id=1, replica_groups=mesh['row'=16,'col'=16] {'row'}, dimensions={0} | all-to-all | bytes 524288 | tf_op jit(solution)/shard_map/all_to_all | solution.py:251
  48.0 2.1 %collective-permute-done.5.other_ref = f32[1280,128]{1,0:T(8,128)S(1)} collective-permute-done((f32[1280,128]{1,0:T(8,128)S(1)}, f32[1280,128]{1,0:T(8,128)S(1)}, u32[]{:S(2)}, u32[]{:S(2)}) %collective-permute-start.5) | collective-permute-done | bytes 655392 | tf_op jit(solution)/shard_map/ppermute | solution.py:278
  50.0 3.2 %wide.1 = f32[256,1024]{1,0:T(8,128)} custom-call(s32[1]{0:T(128)} %bitcast.column, f32[1280,128]{1,0:T(8,128)S(1)} %add_add_fusion.mine_ref, f32[1280,128]{1,0:T(8,128)S(1)} %collective-permute-done.5.other_ref, bf16[1280,1024]{1,0:T(8,128)(2,1)S(1)} %copy-done.2, bf16[1280,1024]{1,0:T(8,128)(2,1)S(1)} %copy-done.3), custom_call_target="tpu_custom_call" | custom-call | flops 6000000000 | bytes 6000000 | tf_op jit(solution)/shard_map/wide/pallas_call | solution.py:212
  53.3 6.2 %all-to-all-start.2 = ((f32[16,16,1024]{2,1,0:T(8,128)}), f32[16,16,1024]{2,1,0:T(8,128)S(1)}, u32[]{:S(2)}, u32[]{:S(2)}) async-start(f32[16,16,1024]{2,1,0:T(8,128)} %bitcast.7), calls=%async_computation.2 | async-start | bytes 2097152 | tf_op jit(solution)/shard_map/all_to_all | solution.py:251
  59.5 11.2 %factor.1 = f32[3,128,128]{2,1,0:T(8,128)S(1)} custom-call(s32[1]{0:T(128)} %bitcast.column, f32[256,256]{1,0:T(8,128)S(1)} %bitcast.22), custom_call_target="tpu_custom_call" | custom-call | flops 12000000000 | bytes 12000000 | tf_op jit(solution)/shard_map/factor/pallas_call | solution.py:212
  70.7 3.4 %collective-permute-start.7 = (f32[3,128,128]{2,1,0:T(8,128)S(1)}, f32[3,128,128]{2,1,0:T(8,128)S(1)}, u32[]{:S(2)}, u32[]{:S(2)}) collective-permute-start(f32[3,128,128]{2,1,0:T(8,128)S(1)} %factor.1), channel_id=1, source_target_pairs={{0,10},{1,11},{16,26},{17,27},{32,42},{33,43},{48,58},{49,59},{64,... | collective-permute-start | bytes 589832 | tf_op jit(solution)/shard_map/ppermute | solution.py:234
  74.1 1.4 %collective-permute-start.6 = (f32[3,128,128]{2,1,0:T(8,128)S(1)}, f32[3,128,128]{2,1,0:T(8,128)S(1)}, u32[]{:S(2)}, u32[]{:S(2)}) collective-permute-start(f32[3,128,128]{2,1,0:T(8,128)S(1)} %factor.1), channel_id=1, source_target_pairs={{0,6},{1,7},{16,22},{17,23},{32,38},{33,39},{48,54},{49,55},{64,70... | collective-permute-start | bytes 589832 | tf_op jit(solution)/shard_map/ppermute | solution.py:234
  76.7 7.2 %all-to-all-start.3 = ((f32[16,16,1024]{2,1,0:T(8,128)}), f32[16,16,1024]{2,1,0:T(8,128)}, u32[]{:S(2)}, u32[]{:S(2)}) async-start(f32[16,16,1024]{2,1,0:T(8,128)} %bitcast.9), calls=%async_computation.3 | async-start | bytes 2097152 | tf_op jit(solution)/shard_map/all_to_all | solution.py:251
  84.0 2.9 %collective-permute-start.9 = (f32[3,128,128]{2,1,0:T(8,128)S(1)}, f32[3,128,128]{2,1,0:T(8,128)S(1)}, u32[]{:S(2)}, u32[]{:S(2)}) collective-permute-start(f32[3,128,128]{2,1,0:T(8,128)S(1)} %add_add_fusion.3), channel_id=1, source_target_pairs={{0,14},{1,15},{6,4},{7,5},{16,30},{17,31},{22,20},{23,21},{32,46},... | collective-permute-start | bytes 589832 | tf_op jit(solution)/shard_map/ppermute | solution.py:234
  86.9 1.3 %collective-permute-start.8 = (f32[3,128,128]{2,1,0:T(8,128)S(1)}, f32[3,128,128]{2,1,0:T(8,128)S(1)}, u32[]{:S(2)}, u32[]{:S(2)}) collective-permute-start(f32[3,128,128]{2,1,0:T(8,128)S(1)} %add_add_fusion.3), channel_id=1, source_target_pairs={{0,2},{1,3},{6,8},{7,9},{10,12},{11,13},{16,18},{17,19},{22,24},{2... | collective-permute-start | bytes 589832 | tf_op jit(solution)/shard_map/ppermute | solution.py:234
  88.2 1.8 %collective-permute-done.9 = f32[3,128,128]{2,1,0:T(8,128)S(1)} collective-permute-done((f32[3,128,128]{2,1,0:T(8,128)S(1)}, f32[3,128,128]{2,1,0:T(8,128)S(1)}, u32[]{:S(2)}, u32[]{:S(2)}) %collective-permute-start.9) | collective-permute-done | bytes 196640 | tf_op jit(solution)/shard_map/ppermute | solution.py:234
  90.0 1.3 %collective-permute-done.8 = f32[3,128,128]{2,1,0:T(8,128)S(1)} collective-permute-done((f32[3,128,128]{2,1,0:T(8,128)S(1)}, f32[3,128,128]{2,1,0:T(8,128)S(1)}, u32[]{:S(2)}, u32[]{:S(2)}) %collective-permute-start.8) | collective-permute-done | bytes 196640 | tf_op jit(solution)/shard_map/ppermute | solution.py:234
  93.9 5.4 %all-to-all-done.3 = f32[16,16,1024]{2,1,0:T(8,128)} async-done(((f32[16,16,1024]{2,1,0:T(8,128)}), f32[16,16,1024]{2,1,0:T(8,128)}, u32[]{:S(2)}, u32[]{:S(2)}) %all-to-all-start.3) | async-done | bytes 1048608 | tf_op jit(solution)/shard_map/all_to_all | solution.py:251
  99.3 8.7 %finish.1 = (f32[10240,128]{1,0:T(8,128)}, f32[2048,128]{1,0:T(8,128)}) custom-call(s32[1]{0:T(128)} %bitcast.column, bf16[1280,256]{1,0:T(8,128)(2,1)} %copy-done.4, bf16[1280,256]{1,0:T(8,128)(2,1)} %copy-done.5, f32[10240,128]{1,0:T(8,128)} %bitcast.25, f32[256,1024]{1,0:T(8,128)} %bitcast.10.w_ref, f32[3,128,128]{2,1,0:T(8,128)} %copy-done), custom_call_target="tpu_custom_call" | custom-call | flops 6000000000 | bytes 6000000 | tf_op jit(solution)/shard_map/finish/pallas_call | solution.py:212
  (28 shorter events, 4.6 us)
Async XLA Ops:
  3.4 10.8 %collective-permute-start = (f32[1280,128]{1,0:T(8,128)S(1)}, f32[1280,128]{1,0:T(8,128)S(1)}, u32[]{:S(2)}, u32[]{:S(2)}) collective-permute-start(f32[1280,128]{1,0:T(8,128)S(1)} %bitcast.15), channel_id=1, source_target_pairs={{0,1},{1,0},{16,17},{17,16},{32,33},{33,32},{48,49},{49,48},{64,65... | collective-permute-start | bytes 1966088 | tf_op jit(solution)/shard_map/ppermute | solution.py:264
  5.3 25.0 %collective-permute-start.2 = (f32[1280,128]{1,0:T(8,128)S(1)}, f32[1280,128]{1,0:T(8,128)S(1)}, u32[]{:S(2)}, u32[]{:S(2)}) collective-permute-start(f32[1280,128]{1,0:T(8,128)S(1)} %bitcast.16), channel_id=1, source_target_pairs={{0,10},{1,11},{16,26},{17,27},{32,42},{33,43},{48,58},{49,59},{64,... | collective-permute-start | bytes 1966088 | tf_op jit(solution)/shard_map/ppermute | solution.py:234
  12.8 17.5 %collective-permute-start.1 = (f32[1280,128]{1,0:T(8,128)S(1)}, f32[1280,128]{1,0:T(8,128)S(1)}, u32[]{:S(2)}, u32[]{:S(2)}) collective-permute-start(f32[1280,128]{1,0:T(8,128)S(1)} %bitcast.17), channel_id=1, source_target_pairs={{0,6},{1,7},{16,22},{17,23},{32,38},{33,39},{48,54},{49,55},{64,70... | collective-permute-start | bytes 1966088 | tf_op jit(solution)/shard_map/ppermute | solution.py:234
  16.2 14.8 %all-to-all-start = ((f32[16,16,256]{2,1,0:T(8,128)}), f32[16,16,256]{2,1,0:T(8,128)S(1)}, u32[]{:S(2)}, u32[]{:S(2)}) async-start(f32[16,16,256]{2,1,0:T(8,128)} %bitcast.2), calls=%async_computation | async-start | bytes 524288 | tf_op jit(solution)/shard_map/all_to_all | solution.py:251
  28.8 1.5 %copy-start.1 = (bf16[1280,1024]{1,0:T(8,128)(2,1)}, bf16[1280,1024]{1,0:T(8,128)(2,1)S(1)}, u32[]{:S(2)}) copy-start(bf16[1280,1024]{1,0:T(8,128)(2,1)S(1)} %get-tuple-element.22.high_ref) | copy-start | bytes 7864324
  31.0 19.0 %copy-start.2 = (bf16[1280,1024]{1,0:T(8,128)(2,1)S(1)}, bf16[1280,1024]{1,0:T(8,128)(2,1)}, u32[]{:S(2)}) copy-start(bf16[1280,1024]{1,0:T(8,128)(2,1)} %copy-done.1) | copy-start | bytes 7864324
  31.0 19.0 %copy-start.3 = (bf16[1280,1024]{1,0:T(8,128)(2,1)S(1)}, bf16[1280,1024]{1,0:T(8,128)(2,1)}, u32[]{:S(2)}) copy-start(bf16[1280,1024]{1,0:T(8,128)(2,1)} %get-tuple-element.23.low_ref) | copy-start | bytes 7864324
  31.0 16.7 %collective-permute-start.4 = (f32[1280,128]{1,0:T(8,128)S(1)}, f32[1280,128]{1,0:T(8,128)S(1)}, u32[]{:S(2)}, u32[]{:S(2)}) collective-permute-start(f32[1280,128]{1,0:T(8,128)S(1)} %add_add_fusion.1), channel_id=1, source_target_pairs={{0,14},{1,15},{6,4},{7,5},{16,30},{17,31},{22,20},{23,21},{32,46},... | collective-permute-start | bytes 1966088 | tf_op jit(solution)/shard_map/ppermute | solution.py:234
  32.6 15.1 %collective-permute-start.3 = (f32[1280,128]{1,0:T(8,128)S(1)}, f32[1280,128]{1,0:T(8,128)S(1)}, u32[]{:S(2)}, u32[]{:S(2)}) collective-permute-start(f32[1280,128]{1,0:T(8,128)S(1)} %add_add_fusion.1), channel_id=1, source_target_pairs={{0,2},{1,3},{6,8},{7,9},{10,12},{11,13},{16,18},{17,19},{22,24},{2... | collective-permute-start | bytes 1966088 | tf_op jit(solution)/shard_map/ppermute | solution.py:234
  47.9 2.2 %collective-permute-start.5 = (f32[1280,128]{1,0:T(8,128)S(1)}, f32[1280,128]{1,0:T(8,128)S(1)}, u32[]{:S(2)}, u32[]{:S(2)}) collective-permute-start(f32[1280,128]{1,0:T(8,128)S(1)} %add_add_fusion.mine_ref), channel_id=1, source_target_pairs={{0,1},{1,0},{2,3},{3,2},{4,5},{5,4},{6,7},{7,6},{8,9},{9,8},{10,11... | collective-permute-start | bytes 1966088 | tf_op jit(solution)/shard_map/ppermute | solution.py:278
  53.3 22.3 %all-to-all-start.2 = ((f32[16,16,1024]{2,1,0:T(8,128)}), f32[16,16,1024]{2,1,0:T(8,128)S(1)}, u32[]{:S(2)}, u32[]{:S(2)}) async-start(f32[16,16,1024]{2,1,0:T(8,128)} %bitcast.7), calls=%async_computation.2 | async-start | bytes 2097152 | tf_op jit(solution)/shard_map/all_to_all | solution.py:251
  70.7 13.2 %collective-permute-start.7 = (f32[3,128,128]{2,1,0:T(8,128)S(1)}, f32[3,128,128]{2,1,0:T(8,128)S(1)}, u32[]{:S(2)}, u32[]{:S(2)}) collective-permute-start(f32[3,128,128]{2,1,0:T(8,128)S(1)} %factor.1), channel_id=1, source_target_pairs={{0,10},{1,11},{16,26},{17,27},{32,42},{33,43},{48,58},{49,59},{64,... | collective-permute-start | bytes 589832 | tf_op jit(solution)/shard_map/ppermute | solution.py:234
  74.1 9.8 %collective-permute-start.6 = (f32[3,128,128]{2,1,0:T(8,128)S(1)}, f32[3,128,128]{2,1,0:T(8,128)S(1)}, u32[]{:S(2)}, u32[]{:S(2)}) collective-permute-start(f32[3,128,128]{2,1,0:T(8,128)S(1)} %factor.1), channel_id=1, source_target_pairs={{0,6},{1,7},{16,22},{17,23},{32,38},{33,39},{48,54},{49,55},{64,70... | collective-permute-start | bytes 589832 | tf_op jit(solution)/shard_map/ppermute | solution.py:234
  76.7 22.6 %all-to-all-start.3 = ((f32[16,16,1024]{2,1,0:T(8,128)}), f32[16,16,1024]{2,1,0:T(8,128)}, u32[]{:S(2)}, u32[]{:S(2)}) async-start(f32[16,16,1024]{2,1,0:T(8,128)} %bitcast.9), calls=%async_computation.3 | async-start | bytes 2097152 | tf_op jit(solution)/shard_map/all_to_all | solution.py:251
  84.0 6.1 %collective-permute-start.9 = (f32[3,128,128]{2,1,0:T(8,128)S(1)}, f32[3,128,128]{2,1,0:T(8,128)S(1)}, u32[]{:S(2)}, u32[]{:S(2)}) collective-permute-start(f32[3,128,128]{2,1,0:T(8,128)S(1)} %add_add_fusion.3), channel_id=1, source_target_pairs={{0,14},{1,15},{6,4},{7,5},{16,30},{17,31},{22,20},{23,21},{32,46},... | collective-permute-start | bytes 589832 | tf_op jit(solution)/shard_map/ppermute | solution.py:234
  86.9 4.5 %collective-permute-start.8 = (f32[3,128,128]{2,1,0:T(8,128)S(1)}, f32[3,128,128]{2,1,0:T(8,128)S(1)}, u32[]{:S(2)}, u32[]{:S(2)}) collective-permute-start(f32[3,128,128]{2,1,0:T(8,128)S(1)} %add_add_fusion.3), channel_id=1, source_target_pairs={{0,2},{1,3},{6,8},{7,9},{10,12},{11,13},{16,18},{17,19},{22,24},{2... | collective-permute-start | bytes 589832 | tf_op jit(solution)/shard_map/ppermute | solution.py:234
  91.4 7.9 %copy-start = (f32[3,128,128]{2,1,0:T(8,128)}, f32[3,128,128]{2,1,0:T(8,128)S(1)}, u32[]{:S(2)}) copy-start(f32[3,128,128]{2,1,0:T(8,128)S(1)} %add_add_fusion.2.x_ref) | copy-start | bytes 589828
  92.2 0.9 copy-start.4
  93.1 0.9 copy-start.5

commit v3 on v2

--- a/solution.py
+++ b/solution.py
@@ -14,7 +14,7 @@
 LANES = 128
 SUB = 8
 RANKS = 16
-BUDGET = dict(gram=16, halves=50, wide=32, total=16, factor=16, basis=24, finish=54)
+BUDGET = dict(gram=16, halves=60, wide=50, total=16, factor=16, basis=24, finish=60)
 
 
 def split(x):
@@ -52,12 +52,12 @@
         high_ref[:, here], low_ref[:, here] = split(m_ref[pl.ds(k, high_ref.shape[0], stride=blocks), :])
 
 
-def wide_kernel(column, mine_ref, other_ref, high_ref, low_ref, out_ref):
-    left = split(panels_of(lax.rem(column[0], 2) == 1, mine_ref, other_ref).T)
-    step = 2 * LANES
-    for k in range(0, out_ref.shape[1], step):
-        here = slice(k, k + step)
-        out_ref[:, here] = dot3(left, (high_ref[:, here], low_ref[:, here]))
+def wide_kernel(column, mine_ref, other_ref, high_ref, low_ref, out_ref, left_ref):
+    @pl.when(pl.program_id(0) == 0)
+    def _():
+        left_ref[0], left_ref[1] = split(panels_of(lax.rem(column[0], 2) == 1, mine_ref, other_ref).T)
+
+    out_ref[...] = dot3((left_ref[0], left_ref[1]), (high_ref[...], low_ref[...]))
 
 
 def total_kernel(column, part_ref, out_ref):
@@ -156,59 +156,80 @@
 
 
 def final_kernel(
-    scale, column, high_ref, low_ref, m_ref, w_ref, x_ref, factors_ref, upper_ref, coef_ref, ch_ref, cl_ref
+    scale, chunks, column, high_in, low_in, m_in, w_in, x_in, factors_out, upper_out,
+    high_ref, low_ref, m_ref, w_ref, x_ref, up_ref, ch_ref, cl_ref, small_sem, in_sem, out_sem, up_sem,
 ):
-    rows = high_ref.shape[0]
-    blocks = m_ref.shape[0] // rows
+    all_rows = high_ref.shape[0]
+    rows = all_rows // chunks
+    blocks = m_ref.shape[0] // all_rows
     place = column[0]
     n = LANES
     owner = place < 2
-    turn = pl.program_id(0)
-
-    @pl.when(turn == 0)
-    def _():
-        inverse = split(whole_inverse(x_ref))
-        unit = lax.broadcasted_iota(jnp.int32, (2 * n, n), 0) == lax.broadcasted_iota(jnp.int32, (2 * n, n), 1) + place * n
-        unit = jnp.where(unit, -scale, 0.0)
+    copy = pltpu.make_async_copy
+    piece = lambda i: pl.ds(i * rows * blocks, rows * blocks)
+    small = [
+        copy(src, dst, small_sem.at[i])
+        for i, (src, dst) in enumerate(((x_in, x_ref), (w_in, w_ref), (high_in, high_ref), (low_in, low_ref)))
+    ]
+    for c in small:
+        c.start()
+    reads = [copy(m_in.at[piece(i), :], m_ref.at[piece(i), :], in_sem.at[i]) for i in range(chunks)]
+    writes = [copy(m_ref.at[piece(i), :], factors_out.at[piece(i), :], out_sem.at[i]) for i in range(chunks)]
+    for c in reads:
+        c.start()
+    small[0].wait()
+    inverse = split(whole_inverse(x_ref))
+    unit = lax.broadcasted_iota(jnp.int32, (2 * n, n), 0) == lax.broadcasted_iota(jnp.int32, (2 * n, n), 1) + place * n
+    unit = jnp.where(unit, -scale, 0.0)
+    small[1].wait()
+    for k in range(0, blocks, 2):
+        here = slice(k * n, (k + 2) * n)
+        coef = dot3(inverse, split(w_ref[:, here]))
+        for j in range(2):
+            up_ref[pl.ds(k + j, 2 * n, stride=blocks), :] = coef[:, j * n : (j + 1) * n] * (1.0 / scale)
+        if k == 0:
+            coef = jnp.concatenate([jnp.where(owner, unit, coef[:, 0:n]), coef[:, n : 2 * n]], axis=1)
+        ch_ref[:, here], cl_ref[:, here] = split(coef)
+    upper = copy(up_ref, upper_out, up_sem)
+    upper.start()
+    small[2].wait()
+    small[3].wait()
+    for i in range(chunks):
+        basis = high_ref[i * rows : (i + 1) * rows, :], low_ref[i * rows : (i + 1) * rows, :]
+        reads[i].wait()
         for k in range(0, blocks, 2):
             here = slice(k * n, (k + 2) * n)
-            coef = dot3(inverse, split(w_ref[:, here]))
-            coef_ref[:, here] = coef * (1.0 / scale)
-            if k == 0:
-                coef = jnp.concatenate([jnp.where(owner, unit, coef[:, 0:n]), coef[:, n : 2 * n]], axis=1)
-            ch_ref[:, here], cl_ref[:, here] = split(coef)
-
-    basis = high_ref[...], low_ref[...]
-    for k in range(0, blocks, 2):
-        here = slice(k * n, (k + 2) * n)
-        change = dot3(basis, (ch_ref[:, here], cl_ref[:, here]))
-        left = m_ref[pl.ds(k, rows, stride=blocks), :]
-        if k == 0:
-            left = jnp.where(owner, 0.0, left)
-        factors_ref[pl.ds(k, rows, stride=blocks), :] = left - change[:, 0:n]
-        factors_ref[pl.ds(k + 1, rows, stride=blocks), :] = (
-            m_ref[pl.ds(k + 1, rows, stride=blocks), :] - change[:, n : 2 * n]
-        )
-    some = upper_ref.shape[0] // blocks
-    for k in range(blocks):
-        upper_ref[pl.ds(k, some, stride=blocks), :] = coef_ref[
-            pl.ds(pl.multiple_of(turn * some, some), some), k * n : (k + 1) * n
-        ]
+            change = dot3(basis, (ch_ref[:, here], cl_ref[:, here]))
+            for j in range(2):
+                at = pl.ds(i * rows * blocks + k + j, rows, stride=blocks)
+                old = m_ref[at, :]
+                if k + j == 0:
+                    old = jnp.where(owner, 0.0, old)
+                m_ref[at, :] = old - change[:, j * n : (j + 1) * n]
+        writes[i].start()
+    upper.wait()
+    for c in writes:
+        c.wait()
 
 
 IN_SMEM = pl.BlockSpec(memory_space=pltpu.SMEM)
+ANYWHERE = pl.BlockSpec(memory_space=pl.ANY)
 
 
 def by_rows(array, steps):
     return pl.BlockSpec((array.shape[0] // steps, array.shape[1]), lambda i: (i, 0))
 
 
+def by_columns(array, steps):
+    return pl.BlockSpec((array.shape[0], array.shape[1] // steps), lambda i: (0, i))
+
+
 def fixed(array):
     return pl.BlockSpec(array.shape, lambda i: (0,) * len(array.shape))
 
 
 def kernel_call(body, name, micros, steps, operands, out_shape, row_split, scratch=()):
-    specs = [by_rows(x, steps) if s else fixed(x) for x, s in zip((*operands[1:], *out_shape), row_split)]
+    specs = [by_rows(x, steps) if s == 1 else ANYWHERE if s == 2 else by_columns(x, steps) if s == 3 else fixed(x) for x, s in zip((*operands[1:], *out_shape), row_split)]
     return pl.pallas_call(
         body,
         grid=(steps,),
@@ -230,6 +251,10 @@
     return [(2 * a + c, 2 * b + c) for a, b in pairs for c in range(2)]
 
 
+def by_core(first, second):
+    return [(2 * a, 2 * b) for a, b in first] + [(2 * a + 1, 2 * b + 1) for a, b in second]
+
+
 def send(x, pairs):
     return lax.ppermute(x, "col", both_cores(pairs))
 
@@ -243,8 +268,8 @@
     return send(x, [(0, 1), (3, 4), (5, 6)]), send(x, [(0, 7), (3, 2)])
 
 
-def total(column, part):
-    return kernel_call(total_kernel, "total", 1, 1, (column, part), (shape(*part.shape),), (0, 0))[0]
+def total(column, part, micros=1):
+    return kernel_call(total_kernel, "total", micros, 1, (column, part), (shape(*part.shape),), (0, 0))[0]
 
 
 def exchange(x):
@@ -264,20 +289,27 @@
     partner = lax.ppermute(lead, "col", [(0, 1), (1, 0)])
     (part,) = kernel_call(gram_kernel, "gram", 3, 1, (column, lead, partner), (shape(n, n),), (0, 0, 0))
     half = jax.ShapeDtypeStruct((rows, blocks * lanes), BF16)
-    later, part = lax.optimization_barrier((column, part))
+    lead, part = lax.optimization_barrier((lead, part))
+    hop = lambda x, first, second: lax.ppermute(x, "col", by_core(first, second))
+    part = exchange(part)
+    first = hop(lead, [(0, 3)], [(0, 5)])
+    held = jnp.where(chip == 0, lead, 0.0) + first
+    part, _ = lax.optimization_barrier((part, held))
+    near = hop(held, [(0, 7), (3, 4)], [(0, 1), (5, 6)]), hop(held, [(3, 2)], [(5, 4)])
+    summed = total(column, part, 30)
+    near, summed = lax.optimization_barrier((near, summed))
+    more = held + near[0] + near[1]
+    gram = exchange(summed)
+    later, _ = lax.optimization_barrier((column, more))
     m_high, m_low = kernel_call(halves_kernel, "halves", 4, steps, (later, m2), (half, half), (1, 1, 1))
-    part = exchange(part)
-    far = send(lead, [(0, 3)]), send(lead, [(0, 5)])
-    far, _, _ = lax.optimization_barrier((far, m_high, m_low))
-    held = jnp.where(chip == 0, lead, 0.0) + far[0] + far[1]
-    part, held = lax.optimization_barrier((part, held))
-    near = spread_near(held)
-    gram = exchange(total(column, part))
-    near, gram = lax.optimization_barrier((near, gram))
-    mine = held + near[0] + near[1]
+    last = hop(more, [(2, 1), (4, 5), (7, 6)], [(6, 7), (4, 3), (1, 2)])
+    last, _, _ = lax.optimization_barrier((last, m_high, m_low))
+    last, gram = lax.optimization_barrier((last, gram))
+    mine = more + last
     other = lax.ppermute(mine, "col", [(i, i ^ 1) for i in range(16)])
     (wide,) = kernel_call(
-        wide_kernel, "wide", 6, 1, (column, mine, other, m_high, m_low), (shape(n, blocks * lanes),), (0,) * 5
+        wide_kernel, "wide", 6, steps, (column, mine, other, m_high, m_low), (shape(n, blocks * lanes),),
+        (0, 0, 3, 3, 3), scratch=[pltpu.VMEM((2, n, rows), BF16)],
     )
     gram, wide = lax.optimization_barrier((gram, wide))
     wide = exchange(wide)
@@ -294,10 +326,17 @@
     high, low = kernel_call(
         basis_kernel, "basis", 2, 1, (column, mine, other, factor), (half, half), (0, 0, 0, 0, 0)
     )
+    chunks = 4
+    dma = pltpu.SemaphoreType.DMA
     factors, upper = kernel_call(
-        functools.partial(final_kernel, scale), "finish", 6, steps,
-        (column, high, low, m2, wide, factor), (shape(*m2.shape), shape(n * blocks, lanes)),
-        (1, 1, 1, 0, 0, 1, 1), scratch=[pltpu.VMEM((n, blocks * lanes), t) for t in (F32, BF16, BF16)],
+        functools.partial(final_kernel, scale, chunks), "finish", 6, 1,
+        (column, high, low, m2, wide, factor), (shape(*m2.shape), shape(n * blocks, lanes)), (2,) * 7,
+        scratch=[
+            pltpu.VMEM((rows, n), BF16), pltpu.VMEM((rows, n), BF16), pltpu.VMEM(m2.shape, F32),
+            pltpu.VMEM((n, blocks * lanes), F32), pltpu.VMEM((3, lanes, lanes), F32),
+            pltpu.VMEM((n * blocks, lanes), F32), pltpu.VMEM((n, blocks * lanes), BF16),
+            pltpu.VMEM((n, blocks * lanes), BF16), dma((4,)), dma((chunks,)), dma((chunks,)), dma(()),
+        ],
     )
     return factors.reshape(matrix.shape), upper.reshape(n, blocks, lanes)
 

time: 109 us -> 113 us (1.037)
  blocking collectives: 13.8 us -> 0 us
  waiting for transfers between devices: 11.3 us -> 24.1 us
  Pallas kernels: 32.3 us -> 35.5 us
  starting transfers between devices: 43.7 us -> 46.9 us
  local copies, waits for them, and re-layouts: 5.95 us -> 4.44 us
    all_to_all x1 -> x0, blocking collectives: 13.8 us -> none  [exchange(): return lax.all_to_all(x, 'row', 0, 0, tiled=True)]
    ppermute x8 -> x4, starting transfers between devices: 20.8 us -> 11.4 us  [send(): return lax.ppermute(x, 'col', both_cores(pairs))]
    all_to_all x3 -> x4, waiting for transfers between devices: 6 us -> 14.5 us  [exchange(): return lax.all_to_all(x, 'row', 0, 0, tiled=True)]
    all_to_all x3 -> x4, starting transfers between devices: 20.9 us -> 27.4 us  [exchange(): return lax.all_to_all(x, 'row', 0, 0, tiled=True)]
    ppermute x0 -> x4, starting transfers between devices: none -> 6.1 us  [shards(): lax.ppermute(x, 'col', by_core(first, second))]
    pallas_call x8, Pallas kernels: 32.3 us -> 35.5 us  [kernel_call(): pl.pallas_call(body, grid=(steps,), out_shape=out_shape, in_specs=[IN_SME...]
    ppermute x0 -> x4, waiting for transfers between devices: none -> 2.19 us  [shards(): lax.ppermute(x, 'col', by_core(first, second))]
    ppermute x1, waiting for transfers between devices: 0.01 us -> 2.06 us  [shards(): partner = lax.ppermute(lead, 'col', [(0, 1), (1, 0)])]
  transfers between devices with their start and end apart: 13 -> 14, of which waited for: 5 -> 9; matrix products, arithmetic and copies ran while one was open for 0% -> 0% of each run, Pallas kernels for 19% -> 18%
where the time goes in v3:
time: 113 us; the launch traced here: 112 us
  starting transfers between devices  46.9 us (42%)
  Pallas kernels  35.5 us (31%)
  waiting for transfers between devices  24.1 us (21%)
  local copies, waits for them, and re-layouts  4.44 us (4%)
    pallas_call x8, Pallas kernels, kernel_call(): pl.pallas_call(body, grid=(steps,), out_shape=out_shape, in_specs=[IN_SME...  35.5 us
    all_to_all x4, starting transfers between devices, exchange(): return lax.all_to_all(x, 'row', 0, 0, tiled=True)  27.4 us
    all_to_all x4, waiting for transfers between devices, exchange(): return lax.all_to_all(x, 'row', 0, 0, tiled=True)  14.5 us
    ppermute x4, starting transfers between devices, send(): return lax.ppermute(x, 'col', both_cores(pairs))  11.4 us
    ppermute x4, starting transfers between devices, shards(): lax.ppermute(x, 'col', by_core(first, second))  6.1 us
    ppermute x4, waiting for transfers between devices, send(): return lax.ppermute(x, 'col', both_cores(pairs))  3.36 us
    slice x1, local copies, waits for them, and re-layouts, shards(): lead = matrix[:, 0, :]  2.73 us
  transfers between devices with their start and end apart: 14, of which 9 were waited for; matrix products, arithmetic and copies ran while one was open for 0% of the time, Pallas kernels for 18%

profile of v3, /device:TPU:2, one launch (start us, length us, event | category | flops | bytes accessed | tf_op | source)
XLA Modules:
  0.0 112.3 jit_solution(645154646265638335)
XLA Ops:
  0.6 2.7 %slice.3 = f32[1280,1,128]{2,1,0:T(1,128)S(1)} slice(f32[1280,8,128]{2,1,0:T(8,128)} %param.1), slice={[0:1280], [0:1], [0:128]} | slice | bytes 1310720 | tf_op jit(solution)/shard_map/slice | solution.py:287
  3.4 1.9 %collective-permute-start = (f32[1280,128]{1,0:T(8,128)S(1)}, f32[1280,128]{1,0:T(8,128)S(1)}, u32[]{:S(2)}, u32[]{:S(2)}) collective-permute-start(f32[1280,128]{1,0:T(8,128)S(1)} %bitcast.15), channel_id=1, source_target_pairs={{0,1},{1,0},{16,17},{17,16},{32,33},{33,32},{48,49},{49,48},{64,65... | collective-permute-start | bytes 1966088 | tf_op jit(solution)/shard_map/ppermute | solution.py:289
  5.3 2.1 %collective-permute-done.other_ref = f32[1280,128]{1,0:T(8,128)S(1)} collective-permute-done((f32[1280,128]{1,0:T(8,128)S(1)}, f32[1280,128]{1,0:T(8,128)S(1)}, u32[]{:S(2)}, u32[]{:S(2)}) %collective-permute-start) | collective-permute-done | bytes 655392 | tf_op jit(solution)/shard_map/ppermute | solution.py:289
  7.4 2.1 %gram.1 = f32[256,256]{1,0:T(8,128)} custom-call(s32[1]{0:T(128)} %bitcast.column, f32[1280,128]{1,0:T(8,128)S(1)} %bitcast.16, f32[1280,128]{1,0:T(8,128)S(1)} %collective-permute-done.other_ref), custom_call_target="tpu_custom_call" | custom-call | flops 3000000000 | bytes 3000000 | tf_op jit(solution)/shard_map/gram/pallas_call | solution.py:233
  9.4 3.3 %collective-permute-start.1 = (f32[1280,128]{1,0:T(8,128)S(1)}, f32[1280,128]{1,0:T(8,128)S(1)}, u32[]{:S(2)}, u32[]{:S(2)}) collective-permute-start(f32[1280,128]{1,0:T(8,128)S(1)} %bitcast.17), channel_id=1, source_target_pairs={{0,6},{1,11},{16,22},{17,27},{32,38},{33,43},{48,54},{49,59},{64,7... | collective-permute-start | bytes 1966088 | tf_op jit(solution)/shard_map/ppermute | solution.py:293
  12.7 7.5 %all-to-all-start = ((f32[16,16,256]{2,1,0:T(8,128)}), f32[16,16,256]{2,1,0:T(8,128)S(1)}, u32[]{:S(2)}, u32[]{:S(2)}) async-start(f32[16,16,256]{2,1,0:T(8,128)} %bitcast.2), calls=%async_computation | async-start | bytes 524288 | tf_op jit(solution)/shard_map/all_to_all | solution.py:276
  21.5 1.4 %collective-permute-start.2 = (f32[1280,128]{1,0:T(8,128)S(1)}, f32[1280,128]{1,0:T(8,128)S(1)}, u32[]{:S(2)}, u32[]{:S(2)}) collective-permute-start(f32[1280,128]{1,0:T(8,128)S(1)} %select_add_fusion), channel_id=1, source_target_pairs={{0,14},{6,8},{1,3},{11,13},{16,30},{22,24},{17,19},{27,29},{32,46}... | collective-permute-start | bytes 1966088 | tf_op jit(solution)/shard_map/ppermute | solution.py:293
  23.0 5.7 %all-to-all-done = f32[16,16,256]{2,1,0:T(8,128)S(1)} async-done(((f32[16,16,256]{2,1,0:T(8,128)}), f32[16,16,256]{2,1,0:T(8,128)S(1)}, u32[]{:S(2)}, u32[]{:S(2)}) %all-to-all-start) | async-done | bytes 262176 | tf_op jit(solution)/shard_map/all_to_all | solution.py:276
  29.4 1.6 %collective-permute-done.2 = f32[1280,128]{1,0:T(8,128)S(1)} collective-permute-done((f32[1280,128]{1,0:T(8,128)S(1)}, f32[1280,128]{1,0:T(8,128)S(1)}, u32[]{:S(2)}, u32[]{:S(2)}) %collective-permute-start.2) | collective-permute-done | bytes 655392 | tf_op jit(solution)/shard_map/ppermute | solution.py:293
  31.8 7.4 %all-to-all-start.1 = ((f32[16,16,256]{2,1,0:T(8,128)}), f32[16,16,256]{2,1,0:T(8,128)S(1)}, u32[]{:S(2)}, u32[]{:S(2)}) async-start(f32[16,16,256]{2,1,0:T(8,128)} %bitcast.5), calls=%async_computation.1 | async-start | bytes 524288 | tf_op jit(solution)/shard_map/all_to_all | solution.py:276
  39.2 6.0 %halves.1 = (bf16[1280,1024]{1,0:T(8,128)(2,1)}, bf16[1280,1024]{1,0:T(8,128)(2,1)}) custom-call(s32[1]{0:T(128)} %bitcast.column, f32[10240,128]{1,0:T(8,128)} %bitcast.22), custom_call_target="tpu_custom_call" | custom-call | flops 4000000000 | bytes 4000000 | tf_op jit(solution)/shard_map/halves/pallas_call | solution.py:233
  45.3 2.0 %all-to-all-done.1 = f32[16,16,256]{2,1,0:T(8,128)S(1)} async-done(((f32[16,16,256]{2,1,0:T(8,128)}), f32[16,16,256]{2,1,0:T(8,128)S(1)}, u32[]{:S(2)}, u32[]{:S(2)}) %all-to-all-start.1) | async-done | bytes 262176 | tf_op jit(solution)/shard_map/all_to_all | solution.py:276
  47.4 2.1 %collective-permute-done.5.other_ref = f32[1280,128]{1,0:T(8,128)S(1)} collective-permute-done((f32[1280,128]{1,0:T(8,128)S(1)}, f32[1280,128]{1,0:T(8,128)S(1)}, u32[]{:S(2)}, u32[]{:S(2)}) %collective-permute-start.5) | collective-permute-done | bytes 655392 | tf_op jit(solution)/shard_map/ppermute | solution.py:309
  49.5 6.0 %wide.1 = f32[256,1024]{1,0:T(8,128)} custom-call(s32[1]{0:T(128)} %bitcast.column, f32[1280,128]{1,0:T(8,128)S(1)} %add.28.mine_ref, f32[1280,128]{1,0:T(8,128)S(1)} %collective-permute-done.5.other_ref, bf16[1280,1024]{1,0:T(8,128)(2,1)} %get-tuple-element.27.high_ref, bf16[1280,1024]{1,0:T(8,128)(2,1)} %get-tuple-element.28.low_ref), custom_call_target="tpu_custom_call" | custom-call | flops 6000000000 | bytes 6000000 | tf_op jit(solution)/shard_map/wide/pallas_call | solution.py:233
  55.5 5.2 %all-to-all-start.2 = ((f32[16,16,1024]{2,1,0:T(8,128)}), f32[16,16,1024]{2,1,0:T(8,128)S(1)}, u32[]{:S(2)}, u32[]{:S(2)}) async-start(f32[16,16,1024]{2,1,0:T(8,128)} %bitcast.7), calls=%async_computation.2 | async-start | bytes 2097152 | tf_op jit(solution)/shard_map/all_to_all | solution.py:276
  60.7 11.2 %factor.1 = f32[3,128,128]{2,1,0:T(8,128)S(1)} custom-call(s32[1]{0:T(128)} %bitcast.column, f32[256,256]{1,0:T(8,128)S(1)} %bitcast.20), custom_call_target="tpu_custom_call" | custom-call | flops 12000000000 | bytes 12000000 | tf_op jit(solution)/shard_map/factor/pallas_call | solution.py:233
  72.0 7.3 %collective-permute-start.7 = (f32[3,128,128]{2,1,0:T(8,128)S(1)}, f32[3,128,128]{2,1,0:T(8,128)S(1)}, u32[]{:S(2)}, u32[]{:S(2)}) collective-permute-start(f32[3,128,128]{2,1,0:T(8,128)S(1)} %factor.1), channel_id=1, source_target_pairs={{0,10},{1,11},{16,26},{17,27},{32,42},{33,43},{48,58},{49,59},{64,... | collective-permute-start | bytes 589832 | tf_op jit(solution)/shard_map/ppermute | solution.py:259
  79.3 1.3 %collective-permute-start.6 = (f32[3,128,128]{2,1,0:T(8,128)S(1)}, f32[3,128,128]{2,1,0:T(8,128)S(1)}, u32[]{:S(2)}, u32[]{:S(2)}) collective-permute-start(f32[3,128,128]{2,1,0:T(8,128)S(1)} %factor.1), channel_id=1, source_target_pairs={{0,6},{1,7},{16,22},{17,23},{32,38},{33,39},{48,54},{49,55},{64,70... | collective-permute-start | bytes 589832 | tf_op jit(solution)/shard_map/ppermute | solution.py:259
  81.7 7.2 %all-to-all-start.3 = ((f32[16,16,1024]{2,1,0:T(8,128)}), f32[16,16,1024]{2,1,0:T(8,128)}, u32[]{:S(2)}, u32[]{:S(2)}) async-start(f32[16,16,1024]{2,1,0:T(8,128)} %bitcast.9), calls=%async_computation.3 | async-start | bytes 2097152 | tf_op jit(solution)/shard_map/all_to_all | solution.py:276
  90.3 1.5 %collective-permute-start.8 = (f32[3,128,128]{2,1,0:T(8,128)S(1)}, f32[3,128,128]{2,1,0:T(8,128)S(1)}, u32[]{:S(2)}, u32[]{:S(2)}) collective-permute-start(f32[3,128,128]{2,1,0:T(8,128)S(1)} %add_add_fusion.2), channel_id=1, source_target_pairs={{0,2},{1,3},{6,8},{7,9},{10,12},{11,13},{16,18},{17,19},{22,24},{2... | collective-permute-start | bytes 589832 | tf_op jit(solution)/shard_map/ppermute | solution.py:259
  91.8 2.0 %collective-permute-done.9 = f32[3,128,128]{2,1,0:T(8,128)S(1)} collective-permute-done((f32[3,128,128]{2,1,0:T(8,128)S(1)}, f32[3,128,128]{2,1,0:T(8,128)S(1)}, u32[]{:S(2)}, u32[]{:S(2)}) %collective-permute-start.9) | collective-permute-done | bytes 196640 | tf_op jit(solution)/shard_map/ppermute | solution.py:259
  93.9 1.3 %collective-permute-done.8 = f32[3,128,128]{2,1,0:T(8,128)S(1)} collective-permute-done((f32[3,128,128]{2,1,0:T(8,128)S(1)}, f32[3,128,128]{2,1,0:T(8,128)S(1)}, u32[]{:S(2)}, u32[]{:S(2)}) %collective-permute-start.8) | collective-permute-done | bytes 196640 | tf_op jit(solution)/shard_map/ppermute | solution.py:259
  97.7 6.8 %all-to-all-done.3 = f32[16,16,1024]{2,1,0:T(8,128)} async-done(((f32[16,16,1024]{2,1,0:T(8,128)}), f32[16,16,1024]{2,1,0:T(8,128)}, u32[]{:S(2)}, u32[]{:S(2)}) %all-to-all-start.3) | async-done | bytes 1048608 | tf_op jit(solution)/shard_map/all_to_all | solution.py:276
  104.6 7.6 %finish.1 = (f32[10240,128]{1,0:T(8,128)}, f32[2048,128]{1,0:T(8,128)}) custom-call(s32[1]{0:T(128)} %bitcast.column, bf16[1280,256]{1,0:T(8,128)(2,1)} %copy-done.1, bf16[1280,256]{1,0:T(8,128)(2,1)} %copy-done.2, f32[10240,128]{1,0:T(8,128)} %bitcast.23, f32[256,1024]{1,0:T(8,128)} %bitcast.10.w_in, f32[3,128,128]{2,1,0:T(8,128)} %copy-done), custom_call_target="tpu_custom_call" | custom-call | flops 6000000000 | bytes 6000000 | tf_op jit(solution)/shard_map/finish/pallas_call | solution.py:233
  (24 shorter events, 8.0 us)
Async XLA Ops:
  3.4 4.0 %collective-permute-start = (f32[1280,128]{1,0:T(8,128)S(1)}, f32[1280,128]{1,0:T(8,128)S(1)}, u32[]{:S(2)}, u32[]{:S(2)}) collective-permute-start(f32[1280,128]{1,0:T(8,128)S(1)} %bitcast.15), channel_id=1, source_target_pairs={{0,1},{1,0},{16,17},{17,16},{32,33},{33,32},{48,49},{49,48},{64,65... | collective-permute-start | bytes 1966088 | tf_op jit(solution)/shard_map/ppermute | solution.py:289
  9.4 11.3 %collective-permute-start.1 = (f32[1280,128]{1,0:T(8,128)S(1)}, f32[1280,128]{1,0:T(8,128)S(1)}, u32[]{:S(2)}, u32[]{:S(2)}) collective-permute-start(f32[1280,128]{1,0:T(8,128)S(1)} %bitcast.17), channel_id=1, source_target_pairs={{0,6},{1,11},{16,22},{17,27},{32,38},{33,43},{48,54},{49,59},{64,7... | collective-permute-start | bytes 1966088 | tf_op jit(solution)/shard_map/ppermute | solution.py:293
  12.7 15.9 %all-to-all-start = ((f32[16,16,256]{2,1,0:T(8,128)}), f32[16,16,256]{2,1,0:T(8,128)S(1)}, u32[]{:S(2)}, u32[]{:S(2)}) async-start(f32[16,16,256]{2,1,0:T(8,128)} %bitcast.2), calls=%async_computation | async-start | bytes 524288 | tf_op jit(solution)/shard_map/all_to_all | solution.py:276
  20.8 8.5 %collective-permute-start.3 = (f32[1280,128]{1,0:T(8,128)S(1)}, f32[1280,128]{1,0:T(8,128)S(1)}, u32[]{:S(2)}, u32[]{:S(2)}) collective-permute-start(f32[1280,128]{1,0:T(8,128)S(1)} %select_add_fusion), channel_id=1, source_target_pairs={{6,4},{11,9},{22,20},{27,25},{38,36},{43,41},{54,52},{59,57},{70,6... | collective-permute-start | bytes 1966088 | tf_op jit(solution)/shard_map/ppermute | solution.py:293
  21.5 9.5 %collective-permute-start.2 = (f32[1280,128]{1,0:T(8,128)S(1)}, f32[1280,128]{1,0:T(8,128)S(1)}, u32[]{:S(2)}, u32[]{:S(2)}) collective-permute-start(f32[1280,128]{1,0:T(8,128)S(1)} %select_add_fusion), channel_id=1, source_target_pairs={{0,14},{6,8},{1,3},{11,13},{16,30},{22,24},{17,19},{27,29},{32,46}... | collective-permute-start | bytes 1966088 | tf_op jit(solution)/shard_map/ppermute | solution.py:293
  31.1 14.2 %collective-permute-start.4 = (f32[1280,128]{1,0:T(8,128)S(1)}, f32[1280,128]{1,0:T(8,128)S(1)}, u32[]{:S(2)}, u32[]{:S(2)}) collective-permute-start(f32[1280,128]{1,0:T(8,128)S(1)} %add_add_fusion), channel_id=1, source_target_pairs={{4,2},{8,10},{14,12},{13,15},{9,7},{3,5},{20,18},{24,26},{30,28},{... | collective-permute-start | bytes 1966088 | tf_op jit(solution)/shard_map/ppermute | solution.py:293
  31.8 15.4 %all-to-all-start.1 = ((f32[16,16,256]{2,1,0:T(8,128)}), f32[16,16,256]{2,1,0:T(8,128)S(1)}, u32[]{:S(2)}, u32[]{:S(2)}) async-start(f32[16,16,256]{2,1,0:T(8,128)} %bitcast.5), calls=%async_computation.1 | async-start | bytes 524288 | tf_op jit(solution)/shard_map/all_to_all | solution.py:276
  47.3 2.2 %collective-permute-start.5 = (f32[1280,128]{1,0:T(8,128)S(1)}, f32[1280,128]{1,0:T(8,128)S(1)}, u32[]{:S(2)}, u32[]{:S(2)}) collective-permute-start(f32[1280,128]{1,0:T(8,128)S(1)} %add.28.mine_ref), channel_id=1, source_target_pairs={{0,1},{1,0},{2,3},{3,2},{4,5},{5,4},{6,7},{7,6},{8,9},{9,8},{10,11... | collective-permute-start | bytes 1966088 | tf_op jit(solution)/shard_map/ppermute | solution.py:309
  55.5 25.2 %all-to-all-start.2 = ((f32[16,16,1024]{2,1,0:T(8,128)}), f32[16,16,1024]{2,1,0:T(8,128)S(1)}, u32[]{:S(2)}, u32[]{:S(2)}) async-start(f32[16,16,1024]{2,1,0:T(8,128)} %bitcast.7), calls=%async_computation.2 | async-start | bytes 2097152 | tf_op jit(solution)/shard_map/all_to_all | solution.py:276
  72.0 17.0 %collective-permute-start.7 = (f32[3,128,128]{2,1,0:T(8,128)S(1)}, f32[3,128,128]{2,1,0:T(8,128)S(1)}, u32[]{:S(2)}, u32[]{:S(2)}) collective-permute-start(f32[3,128,128]{2,1,0:T(8,128)S(1)} %factor.1), channel_id=1, source_target_pairs={{0,10},{1,11},{16,26},{17,27},{32,42},{33,43},{48,58},{49,59},{64,... | collective-permute-start | bytes 589832 | tf_op jit(solution)/shard_map/ppermute | solution.py:259
  79.3 9.7 %collective-permute-start.6 = (f32[3,128,128]{2,1,0:T(8,128)S(1)}, f32[3,128,128]{2,1,0:T(8,128)S(1)}, u32[]{:S(2)}, u32[]{:S(2)}) collective-permute-start(f32[3,128,128]{2,1,0:T(8,128)S(1)} %factor.1), channel_id=1, source_target_pairs={{0,6},{1,7},{16,22},{17,23},{32,38},{33,39},{48,54},{49,55},{64,70... | collective-permute-start | bytes 589832 | tf_op jit(solution)/shard_map/ppermute | solution.py:259
  81.7 22.8 %all-to-all-start.3 = ((f32[16,16,1024]{2,1,0:T(8,128)}), f32[16,16,1024]{2,1,0:T(8,128)}, u32[]{:S(2)}, u32[]{:S(2)}) async-start(f32[16,16,1024]{2,1,0:T(8,128)} %bitcast.9), calls=%async_computation.3 | async-start | bytes 2097152 | tf_op jit(solution)/shard_map/all_to_all | solution.py:276
  89.0 4.8 %collective-permute-start.9 = (f32[3,128,128]{2,1,0:T(8,128)S(1)}, f32[3,128,128]{2,1,0:T(8,128)S(1)}, u32[]{:S(2)}, u32[]{:S(2)}) collective-permute-start(f32[3,128,128]{2,1,0:T(8,128)S(1)} %add_add_fusion.2), channel_id=1, source_target_pairs={{0,14},{1,15},{6,4},{7,5},{16,30},{17,31},{22,20},{23,21},{32,46},... | collective-permute-start | bytes 589832 | tf_op jit(solution)/shard_map/ppermute | solution.py:259
  90.3 4.8 %collective-permute-start.8 = (f32[3,128,128]{2,1,0:T(8,128)S(1)}, f32[3,128,128]{2,1,0:T(8,128)S(1)}, u32[]{:S(2)}, u32[]{:S(2)}) collective-permute-start(f32[3,128,128]{2,1,0:T(8,128)S(1)} %add_add_fusion.2), channel_id=1, source_target_pairs={{0,2},{1,3},{6,8},{7,9},{10,12},{11,13},{16,18},{17,19},{22,24},{2... | collective-permute-start | bytes 589832 | tf_op jit(solution)/shard_map/ppermute | solution.py:259
  95.2 9.3 %copy-start = (f32[3,128,128]{2,1,0:T(8,128)}, f32[3,128,128]{2,1,0:T(8,128)S(1)}, u32[]{:S(2)}) copy-start(f32[3,128,128]{2,1,0:T(8,128)S(1)} %add_add_fusion.1.x_ref.x_in) | copy-start | bytes 589828
  96.0 0.9 copy-start.1
  96.9 0.8 copy-start.2

commit v4 on v3

--- a/solution.py
+++ b/solution.py
@@ -14,7 +14,7 @@
 LANES = 128
 SUB = 8
 RANKS = 16
-BUDGET = dict(gram=16, halves=60, wide=50, total=16, factor=16, basis=24, finish=60)
+BUDGET = dict(gram=16, halves=60, wide=32, total=16, factor=16, basis=24, finish=60)
 
 
 def split(x):
@@ -52,12 +52,12 @@
         high_ref[:, here], low_ref[:, here] = split(m_ref[pl.ds(k, high_ref.shape[0], stride=blocks), :])
 
 
-def wide_kernel(column, mine_ref, other_ref, high_ref, low_ref, out_ref, left_ref):
-    @pl.when(pl.program_id(0) == 0)
-    def _():
-        left_ref[0], left_ref[1] = split(panels_of(lax.rem(column[0], 2) == 1, mine_ref, other_ref).T)
-
-    out_ref[...] = dot3((left_ref[0], left_ref[1]), (high_ref[...], low_ref[...]))
+def wide_kernel(column, mine_ref, other_ref, high_ref, low_ref, out_ref):
+    left = split(panels_of(lax.rem(column[0], 2) == 1, mine_ref, other_ref).T)
+    step = 2 * LANES
+    for k in range(0, out_ref.shape[1], step):
+        here = slice(k, k + step)
+        out_ref[:, here] = dot3(left, (high_ref[:, here], low_ref[:, here]))
 
 
 def total_kernel(column, part_ref, out_ref):
@@ -220,16 +220,12 @@
     return pl.BlockSpec((array.shape[0] // steps, array.shape[1]), lambda i: (i, 0))
 
 
-def by_columns(array, steps):
-    return pl.BlockSpec((array.shape[0], array.shape[1] // steps), lambda i: (0, i))
-
-
 def fixed(array):
     return pl.BlockSpec(array.shape, lambda i: (0,) * len(array.shape))
 
 
 def kernel_call(body, name, micros, steps, operands, out_shape, row_split, scratch=()):
-    specs = [by_rows(x, steps) if s == 1 else ANYWHERE if s == 2 else by_columns(x, steps) if s == 3 else fixed(x) for x, s in zip((*operands[1:], *out_shape), row_split)]
+    specs = [by_rows(x, steps) if s == 1 else ANYWHERE if s == 2 else fixed(x) for x, s in zip((*operands[1:], *out_shape), row_split)]
     return pl.pallas_call(
         body,
         grid=(steps,),
@@ -249,10 +245,6 @@
 
 def both_cores(pairs):
     return [(2 * a + c, 2 * b + c) for a, b in pairs for c in range(2)]
-
-
-def by_core(first, second):
-    return [(2 * a, 2 * b) for a, b in first] + [(2 * a + 1, 2 * b + 1) for a, b in second]
 
 
 def send(x, pairs):
@@ -289,27 +281,20 @@
     partner = lax.ppermute(lead, "col", [(0, 1), (1, 0)])
     (part,) = kernel_call(gram_kernel, "gram", 3, 1, (column, lead, partner), (shape(n, n),), (0, 0, 0))
     half = jax.ShapeDtypeStruct((rows, blocks * lanes), BF16)
-    lead, part = lax.optimization_barrier((lead, part))
-    hop = lambda x, first, second: lax.ppermute(x, "col", by_core(first, second))
-    part = exchange(part)
-    first = hop(lead, [(0, 3)], [(0, 5)])
-    held = jnp.where(chip == 0, lead, 0.0) + first
+    later, raw = lax.optimization_barrier((column, part))
+    m_high, m_low = kernel_call(halves_kernel, "halves", 4, steps, (later, m2), (half, half), (1, 1, 1))
+    far = send(lead, [(0, 3)]), send(lead, [(0, 5)])
+    far, _, _, _ = lax.optimization_barrier((far, m_high, m_low, raw))
+    held = jnp.where(chip == 0, lead, 0.0) + far[0] + far[1]
+    near = spread_near(held)
+    part = exchange(raw)
     part, _ = lax.optimization_barrier((part, held))
-    near = hop(held, [(0, 7), (3, 4)], [(0, 1), (5, 6)]), hop(held, [(3, 2)], [(5, 4)])
-    summed = total(column, part, 30)
-    near, summed = lax.optimization_barrier((near, summed))
-    more = held + near[0] + near[1]
-    gram = exchange(summed)
-    later, _ = lax.optimization_barrier((column, more))
-    m_high, m_low = kernel_call(halves_kernel, "halves", 4, steps, (later, m2), (half, half), (1, 1, 1))
-    last = hop(more, [(2, 1), (4, 5), (7, 6)], [(6, 7), (4, 3), (1, 2)])
-    last, _, _ = lax.optimization_barrier((last, m_high, m_low))
-    last, gram = lax.optimization_barrier((last, gram))
-    mine = more + last
+    gram = exchange(total(column, part, 30))
+    near, gram = lax.optimization_barrier((near, gram))
+    mine = held + near[0] + near[1]
     other = lax.ppermute(mine, "col", [(i, i ^ 1) for i in range(16)])
     (wide,) = kernel_call(
-        wide_kernel, "wide", 6, steps, (column, mine, other, m_high, m_low), (shape(n, blocks * lanes),),
-        (0, 0, 3, 3, 3), scratch=[pltpu.VMEM((2, n, rows), BF16)],
+        wide_kernel, "wide", 6, 1, (column, mine, other, m_high, m_low), (shape(n, blocks * lanes),), (0,) * 5
     )
     gram, wide = lax.optimization_barrier((gram, wide))
     wide = exchange(wide)

time: 113 us -> 107 us (0.947)
  blocking collectives: 0 us -> 14.6 us
  waiting for transfers between devices: 24.1 us -> 11 us
  starting transfers between devices: 46.9 us -> 43.3 us
  Pallas kernels: 35.5 us -> 32.1 us
    all_to_all x0 -> x1, blocking collectives: none -> 14.6 us  [exchange(): return lax.all_to_all(x, 'row', 0, 0, tiled=True)]
    ppermute x4 -> x8, starting transfers between devices: 11.4 us -> 20.7 us  [send(): return lax.ppermute(x, 'col', both_cores(pairs))]
    all_to_all x4 -> x3, waiting for transfers between devices: 14.5 us -> 5.95 us  [exchange(): return lax.all_to_all(x, 'row', 0, 0, tiled=True)]
    all_to_all x4 -> x3, starting transfers between devices: 27.4 us -> 20.6 us  [exchange(): return lax.all_to_all(x, 'row', 0, 0, tiled=True)]
    ppermute x4 -> x0, starting transfers between devices: 6.1 us -> none  [shards(): lax.ppermute(x, 'col', by_core(first, second))]
    pallas_call x8, Pallas kernels: 35.5 us -> 32.1 us  [kernel_call(): pl.pallas_call(body, grid=(steps,), out_shape=out_shape, in_specs=[IN_SME...]
    ppermute x4 -> x0, waiting for transfers between devices: 2.19 us -> none  [shards(): lax.ppermute(x, 'col', by_core(first, second))]
    ppermute x1, waiting for transfers between devices: 2.06 us -> 0.01 us  [shards(): partner = lax.ppermute(lead, 'col', [(0, 1), (1, 0)])]
  transfers between devices with their start and end apart: 14 -> 13, of which waited for: 9 -> 4; matrix products, arithmetic and copies ran while one was open for 0% -> 0% of each run, Pallas kernels for 18% -> 20%
where the time goes in v4:
time: 107 us
  starting transfers between devices  43.3 us (40%)
  Pallas kernels  32.1 us (30%)
  blocking collectives  14.6 us (14%)
  waiting for transfers between devices  11 us (10%)
  local copies, waits for them, and re-layouts  4.45 us (4%)
    pallas_call x8, Pallas kernels, kernel_call(): pl.pallas_call(body, grid=(steps,), out_shape=out_shape, in_specs=[IN_SME...  32.1 us
    ppermute x8, starting transfers between devices, send(): return lax.ppermute(x, 'col', both_cores(pairs))  20.7 us
    all_to_all x3, starting transfers between devices, exchange(): return lax.all_to_all(x, 'row', 0, 0, tiled=True)  20.6 us
    all_to_all x1, blocking collectives, exchange(): return lax.all_to_all(x, 'row', 0, 0, tiled=True)  14.6 us
    all_to_all x3, waiting for transfers between devices, exchange(): return lax.all_to_all(x, 'row', 0, 0, tiled=True)  5.95 us
    ppermute x8, waiting for transfers between devices, send(): return lax.ppermute(x, 'col', both_cores(pairs))  2.99 us
    slice x1, local copies, waits for them, and re-layouts, shards(): lead = matrix[:, 0, :]  2.73 us
  transfers between devices with their start and end apart: 13, of which 4 were waited for; matrix products, arithmetic and copies ran while one was open for 0% of the time, Pallas kernels for 20%

profile of v4, /device:TPU:2, one launch (start us, length us, event | category | flops | bytes accessed | tf_op | source)
XLA Modules:
  0.0 106.8 jit_solution(5938476170427436176)
XLA Ops:
  0.6 2.7 %slice.3 = f32[1280,1,128]{2,1,0:T(1,128)S(1)} slice(f32[1280,8,128]{2,1,0:T(8,128)} %param.1), slice={[0:1280], [0:1], [0:128]} | slice | bytes 1310720 | tf_op jit(solution)/shard_map/slice | solution.py:279
  3.4 1.9 %collective-permute-start.2 = (f32[1280,128]{1,0:T(8,128)S(1)}, f32[1280,128]{1,0:T(8,128)S(1)}, u32[]{:S(2)}, u32[]{:S(2)}) collective-permute-start(f32[1280,128]{1,0:T(8,128)S(1)} %bitcast.15), channel_id=1, source_target_pairs={{0,1},{1,0},{16,17},{17,16},{32,33},{33,32},{48,49},{49,48},{64,65... | collective-permute-start | bytes 1966088 | tf_op jit(solution)/shard_map/ppermute | solution.py:281
  5.3 7.5 %collective-permute-start.1 = (f32[1280,128]{1,0:T(8,128)S(1)}, f32[1280,128]{1,0:T(8,128)S(1)}, u32[]{:S(2)}, u32[]{:S(2)}) collective-permute-start(f32[1280,128]{1,0:T(8,128)S(1)} %bitcast.16), channel_id=1, source_target_pairs={{0,10},{1,11},{16,26},{17,27},{32,42},{33,43},{48,58},{49,59},{64,... | collective-permute-start | bytes 1966088 | tf_op jit(solution)/shard_map/ppermute | solution.py:251
  12.8 1.3 %collective-permute-start = (f32[1280,128]{1,0:T(8,128)S(1)}, f32[1280,128]{1,0:T(8,128)S(1)}, u32[]{:S(2)}, u32[]{:S(2)}) collective-permute-start(f32[1280,128]{1,0:T(8,128)S(1)} %bitcast.17), channel_id=1, source_target_pairs={{0,6},{1,7},{16,22},{17,23},{32,38},{33,39},{48,54},{49,55},{64,70... | collective-permute-start | bytes 1966088 | tf_op jit(solution)/shard_map/ppermute | solution.py:251
  14.1 2.1 %gram.1 = f32[256,256]{1,0:T(8,128)} custom-call(s32[1]{0:T(128)} %bitcast.column, f32[1280,128]{1,0:T(8,128)S(1)} %bitcast.18, f32[1280,128]{1,0:T(8,128)S(1)} %collective-permute-done.2.other_ref), custom_call_target="tpu_custom_call" | custom-call | flops 3000000000 | bytes 3000000 | tf_op jit(solution)/shard_map/gram/pallas_call | solution.py:229
  16.2 7.5 %all-to-all-start = ((f32[16,16,256]{2,1,0:T(8,128)}), f32[16,16,256]{2,1,0:T(8,128)S(1)}, u32[]{:S(2)}, u32[]{:S(2)}) async-start(f32[16,16,256]{2,1,0:T(8,128)} %bitcast.3), calls=%async_computation | async-start | bytes 524288 | tf_op jit(solution)/shard_map/all_to_all | solution.py:268
  23.7 6.0 %halves.1 = (bf16[1280,1024]{1,0:T(8,128)(2,1)}, bf16[1280,1024]{1,0:T(8,128)(2,1)}) custom-call(s32[1]{0:T(128)} %bitcast.column, f32[10240,128]{1,0:T(8,128)} %bitcast.24), custom_call_target="tpu_custom_call" | custom-call | flops 4000000000 | bytes 4000000 | tf_op jit(solution)/shard_map/halves/pallas_call | solution.py:229
  29.8 1.3 %collective-permute-start.4 = (f32[1280,128]{1,0:T(8,128)S(1)}, f32[1280,128]{1,0:T(8,128)S(1)}, u32[]{:S(2)}, u32[]{:S(2)}) collective-permute-start(f32[1280,128]{1,0:T(8,128)S(1)} %add_add_fusion.1), channel_id=1, source_target_pairs={{0,14},{1,15},{6,4},{7,5},{16,30},{17,31},{22,20},{23,21},{32,46},... | collective-permute-start | bytes 1966088 | tf_op jit(solution)/shard_map/ppermute | solution.py:251
  31.1 1.3 %collective-permute-start.3 = (f32[1280,128]{1,0:T(8,128)S(1)}, f32[1280,128]{1,0:T(8,128)S(1)}, u32[]{:S(2)}, u32[]{:S(2)}) collective-permute-start(f32[1280,128]{1,0:T(8,128)S(1)} %add_add_fusion.1), channel_id=1, source_target_pairs={{0,2},{1,3},{6,8},{7,9},{10,12},{11,13},{16,18},{17,19},{22,24},{2... | collective-permute-start | bytes 1966088 | tf_op jit(solution)/shard_map/ppermute | solution.py:251
  32.6 14.6 %all_to_all.47 = f32[16,16,256]{2,1,0:T(8,128)S(1)} all-to-all(f32[16,16,256]{2,1,0:T(8,128)S(1)} %bitcast.23), channel_id=1, replica_groups=mesh['row'=16,'col'=16] {'row'}, dimensions={0} | all-to-all | bytes 524288 | tf_op jit(solution)/shard_map/all_to_all | solution.py:268
  47.4 2.1 %collective-permute-done.5.other_ref = f32[1280,128]{1,0:T(8,128)S(1)} collective-permute-done((f32[1280,128]{1,0:T(8,128)S(1)}, f32[1280,128]{1,0:T(8,128)S(1)}, u32[]{:S(2)}, u32[]{:S(2)}) %collective-permute-start.5) | collective-permute-done | bytes 655392 | tf_op jit(solution)/shard_map/ppermute | solution.py:295
  49.5 3.2 %wide.1 = f32[256,1024]{1,0:T(8,128)} custom-call(s32[1]{0:T(128)} %bitcast.column, f32[1280,128]{1,0:T(8,128)S(1)} %add_add_fusion.mine_ref, f32[1280,128]{1,0:T(8,128)S(1)} %collective-permute-done.5.other_ref, bf16[1280,1024]{1,0:T(8,128)(2,1)S(1)} %copy-done.1, bf16[1280,1024]{1,0:T(8,128)(2,1)S(1)} %copy-done.2), custom_call_target="tpu_custom_call" | custom-call | flops 6000000000 | bytes 6000000 | tf_op jit(solution)/shard_map/wide/pallas_call | solution.py:229
  52.7 5.9 %all-to-all-start.2 = ((f32[16,16,1024]{2,1,0:T(8,128)}), f32[16,16,1024]{2,1,0:T(8,128)S(1)}, u32[]{:S(2)}, u32[]{:S(2)}) async-start(f32[16,16,1024]{2,1,0:T(8,128)} %bitcast.7), calls=%async_computation.2 | async-start | bytes 2097152 | tf_op jit(solution)/shard_map/all_to_all | solution.py:268
  58.6 11.2 %factor.1 = f32[3,128,128]{2,1,0:T(8,128)S(1)} custom-call(s32[1]{0:T(128)} %bitcast.column, f32[256,256]{1,0:T(8,128)S(1)} %bitcast.22), custom_call_target="tpu_custom_call" | custom-call | flops 12000000000 | bytes 12000000 | tf_op jit(solution)/shard_map/factor/pallas_call | solution.py:229
  69.8 4.0 %collective-permute-start.7 = (f32[3,128,128]{2,1,0:T(8,128)S(1)}, f32[3,128,128]{2,1,0:T(8,128)S(1)}, u32[]{:S(2)}, u32[]{:S(2)}) collective-permute-start(f32[3,128,128]{2,1,0:T(8,128)S(1)} %factor.1), channel_id=1, source_target_pairs={{0,10},{1,11},{16,26},{17,27},{32,42},{33,43},{48,58},{49,59},{64,... | collective-permute-start | bytes 589832 | tf_op jit(solution)/shard_map/ppermute | solution.py:251
  73.8 1.4 %collective-permute-start.6 = (f32[3,128,128]{2,1,0:T(8,128)S(1)}, f32[3,128,128]{2,1,0:T(8,128)S(1)}, u32[]{:S(2)}, u32[]{:S(2)}) collective-permute-start(f32[3,128,128]{2,1,0:T(8,128)S(1)} %factor.1), channel_id=1, source_target_pairs={{0,6},{1,7},{16,22},{17,23},{32,38},{33,39},{48,54},{49,55},{64,70... | collective-permute-start | bytes 589832 | tf_op jit(solution)/shard_map/ppermute | solution.py:251
  75.3 1.1 %total.3 = f32[256,1024]{1,0:T(8,128)} custom-call(s32[1]{0:T(128)} %bitcast.column, f32[256,1024]{1,0:T(8,128)S(1)} %bitcast.20), custom_call_target="tpu_custom_call" | custom-call | flops 1000000000 | bytes 1000000 | tf_op jit(solution)/shard_map/total/pallas_call | solution.py:229
  76.4 7.2 %all-to-all-start.3 = ((f32[16,16,1024]{2,1,0:T(8,128)}), f32[16,16,1024]{2,1,0:T(8,128)}, u32[]{:S(2)}, u32[]{:S(2)}) async-start(f32[16,16,1024]{2,1,0:T(8,128)} %bitcast.9), calls=%async_computation.3 | async-start | bytes 2097152 | tf_op jit(solution)/shard_map/all_to_all | solution.py:268
  83.7 2.3 %collective-permute-start.9 = (f32[3,128,128]{2,1,0:T(8,128)S(1)}, f32[3,128,128]{2,1,0:T(8,128)S(1)}, u32[]{:S(2)}, u32[]{:S(2)}) collective-permute-start(f32[3,128,128]{2,1,0:T(8,128)S(1)} %add_add_fusion.3), channel_id=1, source_target_pairs={{0,14},{1,15},{6,4},{7,5},{16,30},{17,31},{22,20},{23,21},{32,46},... | collective-permute-start | bytes 589832 | tf_op jit(solution)/shard_map/ppermute | solution.py:251
  86.0 1.5 %collective-permute-start.8 = (f32[3,128,128]{2,1,0:T(8,128)S(1)}, f32[3,128,128]{2,1,0:T(8,128)S(1)}, u32[]{:S(2)}, u32[]{:S(2)}) collective-permute-start(f32[3,128,128]{2,1,0:T(8,128)S(1)} %add_add_fusion.3), channel_id=1, source_target_pairs={{0,2},{1,3},{6,8},{7,9},{10,12},{11,13},{16,18},{17,19},{22,24},{2... | collective-permute-start | bytes 589832 | tf_op jit(solution)/shard_map/ppermute | solution.py:251
  87.5 1.7 %collective-permute-done.9 = f32[3,128,128]{2,1,0:T(8,128)S(1)} collective-permute-done((f32[3,128,128]{2,1,0:T(8,128)S(1)}, f32[3,128,128]{2,1,0:T(8,128)S(1)}, u32[]{:S(2)}, u32[]{:S(2)}) %collective-permute-start.9) | collective-permute-done | bytes 196640 | tf_op jit(solution)/shard_map/ppermute | solution.py:251
  89.2 1.3 %collective-permute-done.8 = f32[3,128,128]{2,1,0:T(8,128)S(1)} collective-permute-done((f32[3,128,128]{2,1,0:T(8,128)S(1)}, f32[3,128,128]{2,1,0:T(8,128)S(1)}, u32[]{:S(2)}, u32[]{:S(2)}) %collective-permute-start.8) | collective-permute-done | bytes 196640 | tf_op jit(solution)/shard_map/ppermute | solution.py:251
  93.0 5.9 %all-to-all-done.3 = f32[16,16,1024]{2,1,0:T(8,128)} async-done(((f32[16,16,1024]{2,1,0:T(8,128)}), f32[16,16,1024]{2,1,0:T(8,128)}, u32[]{:S(2)}, u32[]{:S(2)}) %all-to-all-start.3) | async-done | bytes 1048608 | tf_op jit(solution)/shard_map/all_to_all | solution.py:268
  99.0 7.6 %finish.1 = (f32[10240,128]{1,0:T(8,128)}, f32[2048,128]{1,0:T(8,128)}) custom-call(s32[1]{0:T(128)} %bitcast.column, bf16[1280,256]{1,0:T(8,128)(2,1)} %copy-done.3, bf16[1280,256]{1,0:T(8,128)(2,1)} %copy-done.4, f32[10240,128]{1,0:T(8,128)} %bitcast.25, f32[256,1024]{1,0:T(8,128)} %bitcast.10.w_in, f32[3,128,128]{2,1,0:T(8,128)} %copy-done), custom_call_target="tpu_custom_call" | custom-call | flops 6000000000 | bytes 6000000 | tf_op jit(solution)/shard_map/finish/pallas_call | solution.py:229
  (26 shorter events, 2.9 us)
Async XLA Ops:
  3.4 10.8 %collective-permute-start.2 = (f32[1280,128]{1,0:T(8,128)S(1)}, f32[1280,128]{1,0:T(8,128)S(1)}, u32[]{:S(2)}, u32[]{:S(2)}) collective-permute-start(f32[1280,128]{1,0:T(8,128)S(1)} %bitcast.15), channel_id=1, source_target_pairs={{0,1},{1,0},{16,17},{17,16},{32,33},{33,32},{48,49},{49,48},{64,65... | collective-permute-start | bytes 1966088 | tf_op jit(solution)/shard_map/ppermute | solution.py:281
  5.3 24.4 %collective-permute-start.1 = (f32[1280,128]{1,0:T(8,128)S(1)}, f32[1280,128]{1,0:T(8,128)S(1)}, u32[]{:S(2)}, u32[]{:S(2)}) collective-permute-start(f32[1280,128]{1,0:T(8,128)S(1)} %bitcast.16), channel_id=1, source_target_pairs={{0,10},{1,11},{16,26},{17,27},{32,42},{33,43},{48,58},{49,59},{64,... | collective-permute-start | bytes 1966088 | tf_op jit(solution)/shard_map/ppermute | solution.py:251
  12.8 16.9 %collective-permute-start = (f32[1280,128]{1,0:T(8,128)S(1)}, f32[1280,128]{1,0:T(8,128)S(1)}, u32[]{:S(2)}, u32[]{:S(2)}) collective-permute-start(f32[1280,128]{1,0:T(8,128)S(1)} %bitcast.17), channel_id=1, source_target_pairs={{0,6},{1,7},{16,22},{17,23},{32,38},{33,39},{48,54},{49,55},{64,70... | collective-permute-start | bytes 1966088 | tf_op jit(solution)/shard_map/ppermute | solution.py:251
  16.2 16.3 %all-to-all-start = ((f32[16,16,256]{2,1,0:T(8,128)}), f32[16,16,256]{2,1,0:T(8,128)S(1)}, u32[]{:S(2)}, u32[]{:S(2)}) async-start(f32[16,16,256]{2,1,0:T(8,128)} %bitcast.3), calls=%async_computation | async-start | bytes 524288 | tf_op jit(solution)/shard_map/all_to_all | solution.py:268
  29.8 17.4 %collective-permute-start.4 = (f32[1280,128]{1,0:T(8,128)S(1)}, f32[1280,128]{1,0:T(8,128)S(1)}, u32[]{:S(2)}, u32[]{:S(2)}) collective-permute-start(f32[1280,128]{1,0:T(8,128)S(1)} %add_add_fusion.1), channel_id=1, source_target_pairs={{0,14},{1,15},{6,4},{7,5},{16,30},{17,31},{22,20},{23,21},{32,46},... | collective-permute-start | bytes 1966088 | tf_op jit(solution)/shard_map/ppermute | solution.py:251
  31.1 16.0 %collective-permute-start.3 = (f32[1280,128]{1,0:T(8,128)S(1)}, f32[1280,128]{1,0:T(8,128)S(1)}, u32[]{:S(2)}, u32[]{:S(2)}) collective-permute-start(f32[1280,128]{1,0:T(8,128)S(1)} %add_add_fusion.1), channel_id=1, source_target_pairs={{0,2},{1,3},{6,8},{7,9},{10,12},{11,13},{16,18},{17,19},{22,24},{2... | collective-permute-start | bytes 1966088 | tf_op jit(solution)/shard_map/ppermute | solution.py:251
  32.5 17.0 %copy-start.1 = (bf16[1280,1024]{1,0:T(8,128)(2,1)S(1)}, bf16[1280,1024]{1,0:T(8,128)(2,1)}, u32[]{:S(2)}) copy-start(bf16[1280,1024]{1,0:T(8,128)(2,1)} %get-tuple-element.20.high_ref) | copy-start | bytes 7864324
  32.5 17.0 %copy-start.2 = (bf16[1280,1024]{1,0:T(8,128)(2,1)S(1)}, bf16[1280,1024]{1,0:T(8,128)(2,1)}, u32[]{:S(2)}) copy-start(bf16[1280,1024]{1,0:T(8,128)(2,1)} %get-tuple-element.21.low_ref) | copy-start | bytes 7864324
  47.3 2.2 %collective-permute-start.5 = (f32[1280,128]{1,0:T(8,128)S(1)}, f32[1280,128]{1,0:T(8,128)S(1)}, u32[]{:S(2)}, u32[]{:S(2)}) collective-permute-start(f32[1280,128]{1,0:T(8,128)S(1)} %add_add_fusion.mine_ref), channel_id=1, source_target_pairs={{0,1},{1,0},{2,3},{3,2},{4,5},{5,4},{6,7},{7,6},{8,9},{9,8},{10,11... | collective-permute-start | bytes 1966088 | tf_op jit(solution)/shard_map/ppermute | solution.py:295
  52.7 22.6 %all-to-all-start.2 = ((f32[16,16,1024]{2,1,0:T(8,128)}), f32[16,16,1024]{2,1,0:T(8,128)S(1)}, u32[]{:S(2)}, u32[]{:S(2)}) async-start(f32[16,16,1024]{2,1,0:T(8,128)} %bitcast.7), calls=%async_computation.2 | async-start | bytes 2097152 | tf_op jit(solution)/shard_map/all_to_all | solution.py:268
  69.8 13.8 %collective-permute-start.7 = (f32[3,128,128]{2,1,0:T(8,128)S(1)}, f32[3,128,128]{2,1,0:T(8,128)S(1)}, u32[]{:S(2)}, u32[]{:S(2)}) collective-permute-start(f32[3,128,128]{2,1,0:T(8,128)S(1)} %factor.1), channel_id=1, source_target_pairs={{0,10},{1,11},{16,26},{17,27},{32,42},{33,43},{48,58},{49,59},{64,... | collective-permute-start | bytes 589832 | tf_op jit(solution)/shard_map/ppermute | solution.py:251
  73.8 9.8 %collective-permute-start.6 = (f32[3,128,128]{2,1,0:T(8,128)S(1)}, f32[3,128,128]{2,1,0:T(8,128)S(1)}, u32[]{:S(2)}, u32[]{:S(2)}) collective-permute-start(f32[3,128,128]{2,1,0:T(8,128)S(1)} %factor.1), channel_id=1, source_target_pairs={{0,6},{1,7},{16,22},{17,23},{32,38},{33,39},{48,54},{49,55},{64,70... | collective-permute-start | bytes 589832 | tf_op jit(solution)/shard_map/ppermute | solution.py:251
  76.4 22.6 %all-to-all-start.3 = ((f32[16,16,1024]{2,1,0:T(8,128)}), f32[16,16,1024]{2,1,0:T(8,128)}, u32[]{:S(2)}, u32[]{:S(2)}) async-start(f32[16,16,1024]{2,1,0:T(8,128)} %bitcast.9), calls=%async_computation.3 | async-start | bytes 2097152 | tf_op jit(solution)/shard_map/all_to_all | solution.py:268
  83.7 5.5 %collective-permute-start.9 = (f32[3,128,128]{2,1,0:T(8,128)S(1)}, f32[3,128,128]{2,1,0:T(8,128)S(1)}, u32[]{:S(2)}, u32[]{:S(2)}) collective-permute-start(f32[3,128,128]{2,1,0:T(8,128)S(1)} %add_add_fusion.3), channel_id=1, source_target_pairs={{0,14},{1,15},{6,4},{7,5},{16,30},{17,31},{22,20},{23,21},{32,46},... | collective-permute-start | bytes 589832 | tf_op jit(solution)/shard_map/ppermute | solution.py:251
  86.0 4.5 %collective-permute-start.8 = (f32[3,128,128]{2,1,0:T(8,128)S(1)}, f32[3,128,128]{2,1,0:T(8,128)S(1)}, u32[]{:S(2)}, u32[]{:S(2)}) collective-permute-start(f32[3,128,128]{2,1,0:T(8,128)S(1)} %add_add_fusion.3), channel_id=1, source_target_pairs={{0,2},{1,3},{6,8},{7,9},{10,12},{11,13},{16,18},{17,19},{22,24},{2... | collective-permute-start | bytes 589832 | tf_op jit(solution)/shard_map/ppermute | solution.py:251
  90.5 8.5 %copy-start = (f32[3,128,128]{2,1,0:T(8,128)}, f32[3,128,128]{2,1,0:T(8,128)S(1)}, u32[]{:S(2)}) copy-start(f32[3,128,128]{2,1,0:T(8,128)S(1)} %add_add_fusion.2.x_ref.x_in) | copy-start | bytes 589828
  91.3 0.9 copy-start.3
  92.2 0.8 copy-start.4

commit v5 on v3

--- a/solution.py
+++ b/solution.py
@@ -14,7 +14,7 @@
 LANES = 128
 SUB = 8
 RANKS = 16
-BUDGET = dict(gram=16, halves=60, wide=50, total=16, factor=16, basis=24, finish=60)
+BUDGET = dict(gram=16, wide=50, turn=24, total=16, factor=16, basis=24, finish=60)
 
 
 def split(x):
@@ -45,19 +45,23 @@
     out_ref[...] = dot6(panels.T, panels)
 
 
-def halves_kernel(column, m_ref, high_ref, low_ref):
-    blocks = m_ref.shape[0] // high_ref.shape[0]
-    for k in range(blocks):
-        here = slice(k * LANES, (k + 1) * LANES)
-        high_ref[:, here], low_ref[:, here] = split(m_ref[pl.ds(k, high_ref.shape[0], stride=blocks), :])
-
-
-def wide_kernel(column, mine_ref, other_ref, high_ref, low_ref, out_ref, left_ref):
-    @pl.when(pl.program_id(0) == 0)
-    def _():
-        left_ref[0], left_ref[1] = split(panels_of(lax.rem(column[0], 2) == 1, mine_ref, other_ref).T)
-
-    out_ref[...] = dot3((left_ref[0], left_ref[1]), (high_ref[...], low_ref[...]))
+def turn_kernel(column, mine_ref, out_ref):
+    out_ref[0], out_ref[1] = split(mine_ref[...].T)
+
+
+def wide_kernel(column, mine_ref, other_ref, m_ref, out_ref):
+    rows = other_ref.shape[0]
+    blocks = m_ref.shape[0] // rows
+    swapped = lax.rem(column[0], 2) == 1
+    left = [
+        jnp.concatenate([jnp.where(swapped, other, mine_ref[i]), jnp.where(swapped, mine_ref[i], other)], axis=0)
+        for i, other in enumerate(split(other_ref[...].T))
+    ]
+    for k in range(0, blocks, 2):
+        pair = jnp.concatenate(
+            [m_ref[pl.ds(k, rows, stride=blocks), :], m_ref[pl.ds(k + 1, rows, stride=blocks), :]], axis=1
+        )
+        out_ref[:, k * LANES : (k + 2) * LANES] = dot3(left, split(pair))
 
 
 def total_kernel(column, part_ref, out_ref):
@@ -288,7 +292,6 @@
     n = 2 * lanes
     partner = lax.ppermute(lead, "col", [(0, 1), (1, 0)])
     (part,) = kernel_call(gram_kernel, "gram", 3, 1, (column, lead, partner), (shape(n, n),), (0, 0, 0))
-    half = jax.ShapeDtypeStruct((rows, blocks * lanes), BF16)
     lead, part = lax.optimization_barrier((lead, part))
     hop = lambda x, first, second: lax.ppermute(x, "col", by_core(first, second))
     part = exchange(part)
@@ -300,16 +303,14 @@
     near, summed = lax.optimization_barrier((near, summed))
     more = held + near[0] + near[1]
     gram = exchange(summed)
-    later, _ = lax.optimization_barrier((column, more))
-    m_high, m_low = kernel_call(halves_kernel, "halves", 4, steps, (later, m2), (half, half), (1, 1, 1))
     last = hop(more, [(2, 1), (4, 5), (7, 6)], [(6, 7), (4, 3), (1, 2)])
-    last, _, _ = lax.optimization_barrier((last, m_high, m_low))
-    last, gram = lax.optimization_barrier((last, gram))
     mine = more + last
     other = lax.ppermute(mine, "col", [(i, i ^ 1) for i in range(16)])
+    (turned,) = kernel_call(
+        turn_kernel, "turn", 40, 1, (column, mine), (jax.ShapeDtypeStruct((2, lanes, rows), BF16),), (0, 0)
+    )
     (wide,) = kernel_call(
-        wide_kernel, "wide", 6, steps, (column, mine, other, m_high, m_low), (shape(n, blocks * lanes),),
-        (0, 0, 3, 3, 3), scratch=[pltpu.VMEM((2, n, rows), BF16)],
+        wide_kernel, "wide", 6, 1, (column, turned, other, m2), (shape(n, blocks * lanes),), (0,) * 4
     )
     gram, wide = lax.optimization_barrier((gram, wide))
     wide = exchange(wide)

time: 113 us -> 112 us (level)
  starting transfers between devices: 46.9 us -> 53.9 us
  Pallas kernels: 35.5 us -> 30.1 us
  waiting for transfers between devices: 24.1 us -> 21.7 us
    pallas_call x8, Pallas kernels: 35.5 us -> 30.1 us  [kernel_call(): pl.pallas_call(body, grid=(steps,), out_shape=out_shape, in_specs=[IN_SME...]
    ppermute x4, starting transfers between devices: 11.4 us -> 16.5 us  [send(): return lax.ppermute(x, 'col', both_cores(pairs))]
    all_to_all x4, waiting for transfers between devices: 14.5 us -> 12.5 us  [exchange(): return lax.all_to_all(x, 'row', 0, 0, tiled=True)]
    all_to_all x4, starting transfers between devices: 27.4 us -> 29.4 us  [exchange(): return lax.all_to_all(x, 'row', 0, 0, tiled=True)]
  transfers between devices with their start and end apart: 14 -> 14, of which waited for: 9 -> 8; matrix products, arithmetic and copies ran while one was open for 0% -> 0% of each run, Pallas kernels for 18% -> 18%
where the time goes in v5:
time: 112 us; the launch traced here: 111 us
  starting transfers between devices  53.9 us (48%)
  Pallas kernels  30.1 us (27%)
  waiting for transfers between devices  21.7 us (19%)
  local copies, waits for them, and re-layouts  4.44 us (4%)
    pallas_call x8, Pallas kernels, kernel_call(): pl.pallas_call(body, grid=(steps,), out_shape=out_shape, in_specs=[IN_SME...  30.1 us
    all_to_all x4, starting transfers between devices, exchange(): return lax.all_to_all(x, 'row', 0, 0, tiled=True)  29.4 us
    ppermute x4, starting transfers between devices, send(): return lax.ppermute(x, 'col', both_cores(pairs))  16.5 us
    all_to_all x4, waiting for transfers between devices, exchange(): return lax.all_to_all(x, 'row', 0, 0, tiled=True)  12.5 us
    ppermute x4, starting transfers between devices, shards(): lax.ppermute(x, 'col', by_core(first, second))  6.1 us
    ppermute x4, waiting for transfers between devices, send(): return lax.ppermute(x, 'col', both_cores(pairs))  3.15 us
    slice x1, local copies, waits for them, and re-layouts, shards(): lead = matrix[:, 0, :]  2.73 us
  transfers between devices with their start and end apart: 14, of which 8 were waited for; matrix products, arithmetic and copies ran while one was open for 0% of the time, Pallas kernels for 18%

profile of v5, /device:TPU:2, one launch (start us, length us, event | category | flops | bytes accessed | tf_op | source)
XLA Modules:
  0.0 111.5 jit_solution(13750548618562802898)
XLA Ops:
  0.6 2.7 %slice.3 = f32[1280,1,128]{2,1,0:T(1,128)S(1)} slice(f32[1280,8,128]{2,1,0:T(8,128)} %param.1), slice={[0:1280], [0:1], [0:128]} | slice | bytes 1310720 | tf_op jit(solution)/shard_map/slice | solution.py:291
  3.4 1.9 %collective-permute-start = (f32[1280,128]{1,0:T(8,128)S(1)}, f32[1280,128]{1,0:T(8,128)S(1)}, u32[]{:S(2)}, u32[]{:S(2)}) collective-permute-start(f32[1280,128]{1,0:T(8,128)S(1)} %bitcast.15), channel_id=1, source_target_pairs={{0,1},{1,0},{16,17},{17,16},{32,33},{33,32},{48,49},{49,48},{64,65... | collective-permute-start | bytes 1966088 | tf_op jit(solution)/shard_map/ppermute | solution.py:293
  5.3 2.1 %collective-permute-done.other_ref = f32[1280,128]{1,0:T(8,128)S(1)} collective-permute-done((f32[1280,128]{1,0:T(8,128)S(1)}, f32[1280,128]{1,0:T(8,128)S(1)}, u32[]{:S(2)}, u32[]{:S(2)}) %collective-permute-start) | collective-permute-done | bytes 655392 | tf_op jit(solution)/shard_map/ppermute | solution.py:293
  7.4 2.1 %gram.1 = f32[256,256]{1,0:T(8,128)} custom-call(s32[1]{0:T(128)} %bitcast.column, f32[1280,128]{1,0:T(8,128)S(1)} %bitcast.16, f32[1280,128]{1,0:T(8,128)S(1)} %collective-permute-done.other_ref), custom_call_target="tpu_custom_call" | custom-call | flops 3000000000 | bytes 3000000 | tf_op jit(solution)/shard_map/gram/pallas_call | solution.py:237
  9.4 3.3 %collective-permute-start.1 = (f32[1280,128]{1,0:T(8,128)S(1)}, f32[1280,128]{1,0:T(8,128)S(1)}, u32[]{:S(2)}, u32[]{:S(2)}) collective-permute-start(f32[1280,128]{1,0:T(8,128)S(1)} %bitcast.17), channel_id=1, source_target_pairs={{0,6},{1,11},{16,22},{17,27},{32,38},{33,43},{48,54},{49,59},{64,7... | collective-permute-start | bytes 1966088 | tf_op jit(solution)/shard_map/ppermute | solution.py:296
  12.7 7.5 %all-to-all-start = ((f32[16,16,256]{2,1,0:T(8,128)}), f32[16,16,256]{2,1,0:T(8,128)S(1)}, u32[]{:S(2)}, u32[]{:S(2)}) async-start(f32[16,16,256]{2,1,0:T(8,128)} %bitcast.2), calls=%async_computation | async-start | bytes 524288 | tf_op jit(solution)/shard_map/all_to_all | solution.py:280
  21.5 1.4 %collective-permute-start.2 = (f32[1280,128]{1,0:T(8,128)S(1)}, f32[1280,128]{1,0:T(8,128)S(1)}, u32[]{:S(2)}, u32[]{:S(2)}) collective-permute-start(f32[1280,128]{1,0:T(8,128)S(1)} %select_add_fusion), channel_id=1, source_target_pairs={{0,14},{6,8},{1,3},{11,13},{16,30},{22,24},{17,19},{27,29},{32,46}... | collective-permute-start | bytes 1966088 | tf_op jit(solution)/shard_map/ppermute | solution.py:296
  23.0 5.7 %all-to-all-done = f32[16,16,256]{2,1,0:T(8,128)S(1)} async-done(((f32[16,16,256]{2,1,0:T(8,128)}), f32[16,16,256]{2,1,0:T(8,128)S(1)}, u32[]{:S(2)}, u32[]{:S(2)}) %all-to-all-start) | async-done | bytes 262176 | tf_op jit(solution)/shard_map/all_to_all | solution.py:280
  29.4 1.6 %collective-permute-done.2 = f32[1280,128]{1,0:T(8,128)S(1)} collective-permute-done((f32[1280,128]{1,0:T(8,128)S(1)}, f32[1280,128]{1,0:T(8,128)S(1)}, u32[]{:S(2)}, u32[]{:S(2)}) %collective-permute-start.2) | collective-permute-done | bytes 655392 | tf_op jit(solution)/shard_map/ppermute | solution.py:296
  31.8 7.4 %all-to-all-start.1 = ((f32[16,16,256]{2,1,0:T(8,128)}), f32[16,16,256]{2,1,0:T(8,128)S(1)}, u32[]{:S(2)}, u32[]{:S(2)}) async-start(f32[16,16,256]{2,1,0:T(8,128)} %bitcast.4), calls=%async_computation.1 | async-start | bytes 524288 | tf_op jit(solution)/shard_map/all_to_all | solution.py:280
  39.7 1.8 %collective-permute-done.5.other_ref = f32[1280,128]{1,0:T(8,128)S(1)} collective-permute-done((f32[1280,128]{1,0:T(8,128)S(1)}, f32[1280,128]{1,0:T(8,128)S(1)}, u32[]{:S(2)}, u32[]{:S(2)}) %collective-permute-start.5) | collective-permute-done | bytes 655392 | tf_op jit(solution)/shard_map/ppermute | solution.py:308
  41.5 6.3 %wide.1 = f32[256,1024]{1,0:T(8,128)} custom-call(s32[1]{0:T(128)} %bitcast.column, bf16[2,128,1280]{2,1,0:T(8,128)(2,1)S(1)} %turn.1.mine_ref, f32[1280,128]{1,0:T(8,128)S(1)} %collective-permute-done.5.other_ref, f32[10240,128]{1,0:T(8,128)} %bitcast.22), custom_call_target="tpu_custom_call" | custom-call | flops 6000000000 | bytes 6000000 | tf_op jit(solution)/shard_map/wide/pallas_call | solution.py:237
  47.8 7.2 %all-to-all-start.2 = ((f32[16,16,1024]{2,1,0:T(8,128)}), f32[16,16,1024]{2,1,0:T(8,128)S(1)}, u32[]{:S(2)}, u32[]{:S(2)}) async-start(f32[16,16,1024]{2,1,0:T(8,128)} %bitcast.7), calls=%async_computation.2 | async-start | bytes 2097152 | tf_op jit(solution)/shard_map/all_to_all | solution.py:280
  55.1 11.2 %factor.1 = f32[3,128,128]{2,1,0:T(8,128)S(1)} custom-call(s32[1]{0:T(128)} %bitcast.column, f32[256,256]{1,0:T(8,128)S(1)} %bitcast.20), custom_call_target="tpu_custom_call" | custom-call | flops 12000000000 | bytes 12000000 | tf_op jit(solution)/shard_map/factor/pallas_call | solution.py:237
  66.3 12.4 %collective-permute-start.7 = (f32[3,128,128]{2,1,0:T(8,128)S(1)}, f32[3,128,128]{2,1,0:T(8,128)S(1)}, u32[]{:S(2)}, u32[]{:S(2)}) collective-permute-start(f32[3,128,128]{2,1,0:T(8,128)S(1)} %factor.1), channel_id=1, source_target_pairs={{0,10},{1,11},{16,26},{17,27},{32,42},{33,43},{48,58},{49,59},{64,... | collective-permute-start | bytes 589832 | tf_op jit(solution)/shard_map/ppermute | solution.py:263
  78.7 1.3 %collective-permute-start.6 = (f32[3,128,128]{2,1,0:T(8,128)S(1)}, f32[3,128,128]{2,1,0:T(8,128)S(1)}, u32[]{:S(2)}, u32[]{:S(2)}) collective-permute-start(f32[3,128,128]{2,1,0:T(8,128)S(1)} %factor.1), channel_id=1, source_target_pairs={{0,6},{1,7},{16,22},{17,23},{32,38},{33,39},{48,54},{49,55},{64,70... | collective-permute-start | bytes 589832 | tf_op jit(solution)/shard_map/ppermute | solution.py:263
  80.0 1.1 total.3
  81.1 7.2 %all-to-all-start.3 = ((f32[16,16,1024]{2,1,0:T(8,128)}), f32[16,16,1024]{2,1,0:T(8,128)}, u32[]{:S(2)}, u32[]{:S(2)}) async-start(f32[16,16,1024]{2,1,0:T(8,128)} %bitcast.9), calls=%async_computation.3 | async-start | bytes 2097152 | tf_op jit(solution)/shard_map/all_to_all | solution.py:280
  88.4 1.3 %collective-permute-start.9 = (f32[3,128,128]{2,1,0:T(8,128)S(1)}, f32[3,128,128]{2,1,0:T(8,128)S(1)}, u32[]{:S(2)}, u32[]{:S(2)}) collective-permute-start(f32[3,128,128]{2,1,0:T(8,128)S(1)} %add_add_fusion.2), channel_id=1, source_target_pairs={{0,14},{1,15},{6,4},{7,5},{16,30},{17,31},{22,20},{23,21},{32,46},... | collective-permute-start | bytes 589832 | tf_op jit(solution)/shard_map/ppermute | solution.py:263
  89.7 1.5 %collective-permute-start.8 = (f32[3,128,128]{2,1,0:T(8,128)S(1)}, f32[3,128,128]{2,1,0:T(8,128)S(1)}, u32[]{:S(2)}, u32[]{:S(2)}) collective-permute-start(f32[3,128,128]{2,1,0:T(8,128)S(1)} %add_add_fusion.2), channel_id=1, source_target_pairs={{0,2},{1,3},{6,8},{7,9},{10,12},{11,13},{16,18},{17,19},{22,24},{2... | collective-permute-start | bytes 589832 | tf_op jit(solution)/shard_map/ppermute | solution.py:263
  91.2 1.8 %collective-permute-done.9 = f32[3,128,128]{2,1,0:T(8,128)S(1)} collective-permute-done((f32[3,128,128]{2,1,0:T(8,128)S(1)}, f32[3,128,128]{2,1,0:T(8,128)S(1)}, u32[]{:S(2)}, u32[]{:S(2)}) %collective-permute-start.9) | collective-permute-done | bytes 196640 | tf_op jit(solution)/shard_map/ppermute | solution.py:263
  93.0 1.3 %collective-permute-done.8 = f32[3,128,128]{2,1,0:T(8,128)S(1)} collective-permute-done((f32[3,128,128]{2,1,0:T(8,128)S(1)}, f32[3,128,128]{2,1,0:T(8,128)S(1)}, u32[]{:S(2)}, u32[]{:S(2)}) %collective-permute-start.8) | collective-permute-done | bytes 196640 | tf_op jit(solution)/shard_map/ppermute | solution.py:263
  96.9 6.8 %all-to-all-done.3 = f32[16,16,1024]{2,1,0:T(8,128)} async-done(((f32[16,16,1024]{2,1,0:T(8,128)}), f32[16,16,1024]{2,1,0:T(8,128)}, u32[]{:S(2)}, u32[]{:S(2)}) %all-to-all-start.3) | async-done | bytes 1048608 | tf_op jit(solution)/shard_map/all_to_all | solution.py:280
  103.7 7.6 %finish.1 = (f32[10240,128]{1,0:T(8,128)}, f32[2048,128]{1,0:T(8,128)}) custom-call(s32[1]{0:T(128)} %bitcast.column, bf16[1280,256]{1,0:T(8,128)(2,1)} %copy-done.1, bf16[1280,256]{1,0:T(8,128)(2,1)} %copy-done.2, f32[10240,128]{1,0:T(8,128)} %bitcast.23, f32[256,1024]{1,0:T(8,128)} %bitcast.10.w_in, f32[3,128,128]{2,1,0:T(8,128)} %copy-done), custom_call_target="tpu_custom_call" | custom-call | flops 6000000000 | bytes 6000000 | tf_op jit(solution)/shard_map/finish/pallas_call | solution.py:237
  (24 shorter events, 5.8 us)
Async XLA Ops:
  3.4 4.0 %collective-permute-start = (f32[1280,128]{1,0:T(8,128)S(1)}, f32[1280,128]{1,0:T(8,128)S(1)}, u32[]{:S(2)}, u32[]{:S(2)}) collective-permute-start(f32[1280,128]{1,0:T(8,128)S(1)} %bitcast.15), channel_id=1, source_target_pairs={{0,1},{1,0},{16,17},{17,16},{32,33},{33,32},{48,49},{49,48},{64,65... | collective-permute-start | bytes 1966088 | tf_op jit(solution)/shard_map/ppermute | solution.py:293
  9.4 11.3 %collective-permute-start.1 = (f32[1280,128]{1,0:T(8,128)S(1)}, f32[1280,128]{1,0:T(8,128)S(1)}, u32[]{:S(2)}, u32[]{:S(2)}) collective-permute-start(f32[1280,128]{1,0:T(8,128)S(1)} %bitcast.17), channel_id=1, source_target_pairs={{0,6},{1,11},{16,22},{17,27},{32,38},{33,43},{48,54},{49,59},{64,7... | collective-permute-start | bytes 1966088 | tf_op jit(solution)/shard_map/ppermute | solution.py:296
  12.7 15.9 %all-to-all-start = ((f32[16,16,256]{2,1,0:T(8,128)}), f32[16,16,256]{2,1,0:T(8,128)S(1)}, u32[]{:S(2)}, u32[]{:S(2)}) async-start(f32[16,16,256]{2,1,0:T(8,128)} %bitcast.2), calls=%async_computation | async-start | bytes 524288 | tf_op jit(solution)/shard_map/all_to_all | solution.py:280
  20.8 8.5 %collective-permute-start.3 = (f32[1280,128]{1,0:T(8,128)S(1)}, f32[1280,128]{1,0:T(8,128)S(1)}, u32[]{:S(2)}, u32[]{:S(2)}) collective-permute-start(f32[1280,128]{1,0:T(8,128)S(1)} %select_add_fusion), channel_id=1, source_target_pairs={{6,4},{11,9},{22,20},{27,25},{38,36},{43,41},{54,52},{59,57},{70,6... | collective-permute-start | bytes 1966088 | tf_op jit(solution)/shard_map/ppermute | solution.py:296
  21.5 9.5 %collective-permute-start.2 = (f32[1280,128]{1,0:T(8,128)S(1)}, f32[1280,128]{1,0:T(8,128)S(1)}, u32[]{:S(2)}, u32[]{:S(2)}) collective-permute-start(f32[1280,128]{1,0:T(8,128)S(1)} %select_add_fusion), channel_id=1, source_target_pairs={{0,14},{6,8},{1,3},{11,13},{16,30},{22,24},{17,19},{27,29},{32,46}... | collective-permute-start | bytes 1966088 | tf_op jit(solution)/shard_map/ppermute | solution.py:296
  31.1 8.1 %collective-permute-start.4 = (f32[1280,128]{1,0:T(8,128)S(1)}, f32[1280,128]{1,0:T(8,128)S(1)}, u32[]{:S(2)}, u32[]{:S(2)}) collective-permute-start(f32[1280,128]{1,0:T(8,128)S(1)} %add_add_fusion), channel_id=1, source_target_pairs={{4,2},{8,10},{14,12},{13,15},{9,7},{3,5},{20,18},{24,26},{30,28},{... | collective-permute-start | bytes 1966088 | tf_op jit(solution)/shard_map/ppermute | solution.py:296
  31.8 16.0 %all-to-all-start.1 = ((f32[16,16,256]{2,1,0:T(8,128)}), f32[16,16,256]{2,1,0:T(8,128)S(1)}, u32[]{:S(2)}, u32[]{:S(2)}) async-start(f32[16,16,256]{2,1,0:T(8,128)} %bitcast.4), calls=%async_computation.1 | async-start | bytes 524288 | tf_op jit(solution)/shard_map/all_to_all | solution.py:280
  39.3 2.2 %collective-permute-start.5 = (f32[1280,128]{1,0:T(8,128)S(1)}, f32[1280,128]{1,0:T(8,128)S(1)}, u32[]{:S(2)}, u32[]{:S(2)}) collective-permute-start(f32[1280,128]{1,0:T(8,128)S(1)} %add.28.mine_ref), channel_id=1, source_target_pairs={{0,1},{1,0},{2,3},{3,2},{4,5},{5,4},{6,7},{7,6},{8,9},{9,8},{10,11... | collective-permute-start | bytes 1966088 | tf_op jit(solution)/shard_map/ppermute | solution.py:308
  47.8 32.2 %all-to-all-start.2 = ((f32[16,16,1024]{2,1,0:T(8,128)}), f32[16,16,1024]{2,1,0:T(8,128)S(1)}, u32[]{:S(2)}, u32[]{:S(2)}) async-start(f32[16,16,1024]{2,1,0:T(8,128)} %bitcast.7), calls=%async_computation.2 | async-start | bytes 2097152 | tf_op jit(solution)/shard_map/all_to_all | solution.py:280
  66.3 22.0 %collective-permute-start.7 = (f32[3,128,128]{2,1,0:T(8,128)S(1)}, f32[3,128,128]{2,1,0:T(8,128)S(1)}, u32[]{:S(2)}, u32[]{:S(2)}) collective-permute-start(f32[3,128,128]{2,1,0:T(8,128)S(1)} %factor.1), channel_id=1, source_target_pairs={{0,10},{1,11},{16,26},{17,27},{32,42},{33,43},{48,58},{49,59},{64,... | collective-permute-start | bytes 589832 | tf_op jit(solution)/shard_map/ppermute | solution.py:263
  78.7 9.7 %collective-permute-start.6 = (f32[3,128,128]{2,1,0:T(8,128)S(1)}, f32[3,128,128]{2,1,0:T(8,128)S(1)}, u32[]{:S(2)}, u32[]{:S(2)}) collective-permute-start(f32[3,128,128]{2,1,0:T(8,128)S(1)} %factor.1), channel_id=1, source_target_pairs={{0,6},{1,7},{16,22},{17,23},{32,38},{33,39},{48,54},{49,55},{64,70... | collective-permute-start | bytes 589832 | tf_op jit(solution)/shard_map/ppermute | solution.py:263
  81.1 22.6 %all-to-all-start.3 = ((f32[16,16,1024]{2,1,0:T(8,128)}), f32[16,16,1024]{2,1,0:T(8,128)}, u32[]{:S(2)}, u32[]{:S(2)}) async-start(f32[16,16,1024]{2,1,0:T(8,128)} %bitcast.9), calls=%async_computation.3 | async-start | bytes 2097152 | tf_op jit(solution)/shard_map/all_to_all | solution.py:280
  88.4 4.6 %collective-permute-start.9 = (f32[3,128,128]{2,1,0:T(8,128)S(1)}, f32[3,128,128]{2,1,0:T(8,128)S(1)}, u32[]{:S(2)}, u32[]{:S(2)}) collective-permute-start(f32[3,128,128]{2,1,0:T(8,128)S(1)} %add_add_fusion.2), channel_id=1, source_target_pairs={{0,14},{1,15},{6,4},{7,5},{16,30},{17,31},{22,20},{23,21},{32,46},... | collective-permute-start | bytes 589832 | tf_op jit(solution)/shard_map/ppermute | solution.py:263
  89.7 4.6 %collective-permute-start.8 = (f32[3,128,128]{2,1,0:T(8,128)S(1)}, f32[3,128,128]{2,1,0:T(8,128)S(1)}, u32[]{:S(2)}, u32[]{:S(2)}) collective-permute-start(f32[3,128,128]{2,1,0:T(8,128)S(1)} %add_add_fusion.2), channel_id=1, source_target_pairs={{0,2},{1,3},{6,8},{7,9},{10,12},{11,13},{16,18},{17,19},{22,24},{2... | collective-permute-start | bytes 589832 | tf_op jit(solution)/shard_map/ppermute | solution.py:263
  94.4 9.3 %copy-start = (f32[3,128,128]{2,1,0:T(8,128)}, f32[3,128,128]{2,1,0:T(8,128)S(1)}, u32[]{:S(2)}) copy-start(f32[3,128,128]{2,1,0:T(8,128)S(1)} %add_add_fusion.1.x_ref.x_in) | copy-start | bytes 589828
  95.2 0.9 copy-start.1
  96.1 0.8 copy-start.2

commit v6 on v4

--- a/solution.py
+++ b/solution.py
@@ -283,6 +283,7 @@
     half = jax.ShapeDtypeStruct((rows, blocks * lanes), BF16)
     later, raw = lax.optimization_barrier((column, part))
     m_high, m_low = kernel_call(halves_kernel, "halves", 4, steps, (later, m2), (half, half), (1, 1, 1))
+    lead, raw = lax.optimization_barrier((lead, raw))
     far = send(lead, [(0, 3)]), send(lead, [(0, 5)])
     far, _, _, _ = lax.optimization_barrier((far, m_high, m_low, raw))
     held = jnp.where(chip == 0, lead, 0.0) + far[0] + far[1]

time: 107 us -> 109 us (1.019)
  waiting for transfers between devices: 11 us -> 14.5 us
  starting transfers between devices: 43.3 us -> 41.6 us
    ppermute x1, waiting for transfers between devices: 0.01 us -> 2.06 us  [shards(): partner = lax.ppermute(lead, 'col', [(0, 1), (1, 0)])]
    ppermute x8, starting transfers between devices: 20.7 us -> 19 us  [send(): return lax.ppermute(x, 'col', both_cores(pairs))]
  transfers between devices with their start and end apart: 13 -> 13, of which waited for: 4 -> 6; matrix products, arithmetic and copies ran while one was open for 0% -> 0% of each run, Pallas kernels for 20% -> 18%
where the time goes in v6:
time: 109 us
  starting transfers between devices  41.6 us (38%)
  Pallas kernels  32.1 us (29%)
  blocking collectives  14.9 us (14%)
  waiting for transfers between devices  14.5 us (13%)
  local copies, waits for them, and re-layouts  4.45 us (4%)
    pallas_call x8, Pallas kernels, kernel_call(): pl.pallas_call(body, grid=(steps,), out_shape=out_shape, in_specs=[IN_SME...  32.1 us
    all_to_all x3, starting transfers between devices, exchange(): return lax.all_to_all(x, 'row', 0, 0, tiled=True)  20.6 us
    ppermute x8, starting transfers between devices, send(): return lax.ppermute(x, 'col', both_cores(pairs))  19 us
    all_to_all x1, blocking collectives, exchange(): return lax.all_to_all(x, 'row', 0, 0, tiled=True)  14.9 us
    all_to_all x3, waiting for transfers between devices, exchange(): return lax.all_to_all(x, 'row', 0, 0, tiled=True)  6.82 us
    ppermute x8, waiting for transfers between devices, send(): return lax.ppermute(x, 'col', both_cores(pairs))  3.55 us
    slice x1, local copies, waits for them, and re-layouts, shards(): lead = matrix[:, 0, :]  2.73 us
  transfers between devices with their start and end apart: 13, of which 6 were waited for; matrix products, arithmetic and copies ran while one was open for 0% of the time, Pallas kernels for 18%

profile of v6, /device:TPU:2, one launch (start us, length us, event | category | flops | bytes accessed | tf_op | source)
XLA Modules:
  0.0 108.8 jit_solution(6099882260109263429)
XLA Ops:
  0.6 2.7 %slice.3 = f32[1280,1,128]{2,1,0:T(1,128)S(1)} slice(f32[1280,8,128]{2,1,0:T(8,128)} %param.1), slice={[0:1280], [0:1], [0:128]} | slice | bytes 1310720 | tf_op jit(solution)/shard_map/slice | solution.py:279
  3.4 1.9 %collective-permute-start = (f32[1280,128]{1,0:T(8,128)S(1)}, f32[1280,128]{1,0:T(8,128)S(1)}, u32[]{:S(2)}, u32[]{:S(2)}) collective-permute-start(f32[1280,128]{1,0:T(8,128)S(1)} %bitcast.15), channel_id=1, source_target_pairs={{0,1},{1,0},{16,17},{17,16},{32,33},{33,32},{48,49},{49,48},{64,65... | collective-permute-start | bytes 1966088 | tf_op jit(solution)/shard_map/ppermute | solution.py:281
  5.3 2.1 %collective-permute-done.other_ref = f32[1280,128]{1,0:T(8,128)S(1)} collective-permute-done((f32[1280,128]{1,0:T(8,128)S(1)}, f32[1280,128]{1,0:T(8,128)S(1)}, u32[]{:S(2)}, u32[]{:S(2)}) %collective-permute-start) | collective-permute-done | bytes 655392 | tf_op jit(solution)/shard_map/ppermute | solution.py:281
  7.4 2.1 %gram.1 = f32[256,256]{1,0:T(8,128)} custom-call(s32[1]{0:T(128)} %bitcast.column, f32[1280,128]{1,0:T(8,128)S(1)} %bitcast.16, f32[1280,128]{1,0:T(8,128)S(1)} %collective-permute-done.other_ref), custom_call_target="tpu_custom_call" | custom-call | flops 3000000000 | bytes 3000000 | tf_op jit(solution)/shard_map/gram/pallas_call | solution.py:229
  9.4 5.4 %collective-permute-start.2 = (f32[1280,128]{1,0:T(8,128)S(1)}, f32[1280,128]{1,0:T(8,128)S(1)}, u32[]{:S(2)}, u32[]{:S(2)}) collective-permute-start(f32[1280,128]{1,0:T(8,128)S(1)} %bitcast.17), channel_id=1, source_target_pairs={{0,10},{1,11},{16,26},{17,27},{32,42},{33,43},{48,58},{49,59},{64,... | collective-permute-start | bytes 1966088 | tf_op jit(solution)/shard_map/ppermute | solution.py:251
  14.8 1.3 %collective-permute-start.1 = (f32[1280,128]{1,0:T(8,128)S(1)}, f32[1280,128]{1,0:T(8,128)S(1)}, u32[]{:S(2)}, u32[]{:S(2)}) collective-permute-start(f32[1280,128]{1,0:T(8,128)S(1)} %bitcast.18), channel_id=1, source_target_pairs={{0,6},{1,7},{16,22},{17,23},{32,38},{33,39},{48,54},{49,55},{64,70... | collective-permute-start | bytes 1966088 | tf_op jit(solution)/shard_map/ppermute | solution.py:251
  16.2 7.5 %all-to-all-start = ((f32[16,16,256]{2,1,0:T(8,128)}), f32[16,16,256]{2,1,0:T(8,128)S(1)}, u32[]{:S(2)}, u32[]{:S(2)}) async-start(f32[16,16,256]{2,1,0:T(8,128)} %bitcast.3), calls=%async_computation | async-start | bytes 524288 | tf_op jit(solution)/shard_map/all_to_all | solution.py:268
  23.7 6.0 %halves.1 = (bf16[1280,1024]{1,0:T(8,128)(2,1)}, bf16[1280,1024]{1,0:T(8,128)(2,1)}) custom-call(s32[1]{0:T(128)} %bitcast.column, f32[10240,128]{1,0:T(8,128)} %bitcast.24), custom_call_target="tpu_custom_call" | custom-call | flops 4000000000 | bytes 4000000 | tf_op jit(solution)/shard_map/halves/pallas_call | solution.py:229
  30.2 1.3 %collective-permute-start.4 = (f32[1280,128]{1,0:T(8,128)S(1)}, f32[1280,128]{1,0:T(8,128)S(1)}, u32[]{:S(2)}, u32[]{:S(2)}) collective-permute-start(f32[1280,128]{1,0:T(8,128)S(1)} %add_add_fusion.1), channel_id=1, source_target_pairs={{0,14},{1,15},{6,4},{7,5},{16,30},{17,31},{22,20},{23,21},{32,46},... | collective-permute-start | bytes 1966088 | tf_op jit(solution)/shard_map/ppermute | solution.py:251
  31.5 1.3 %collective-permute-start.3 = (f32[1280,128]{1,0:T(8,128)S(1)}, f32[1280,128]{1,0:T(8,128)S(1)}, u32[]{:S(2)}, u32[]{:S(2)}) collective-permute-start(f32[1280,128]{1,0:T(8,128)S(1)} %add_add_fusion.1), channel_id=1, source_target_pairs={{0,2},{1,3},{6,8},{7,9},{10,12},{11,13},{16,18},{17,19},{22,24},{2... | collective-permute-start | bytes 1966088 | tf_op jit(solution)/shard_map/ppermute | solution.py:251
  33.0 14.9 %all_to_all.47 = f32[16,16,256]{2,1,0:T(8,128)S(1)} all-to-all(f32[16,16,256]{2,1,0:T(8,128)S(1)} %bitcast.23), channel_id=1, replica_groups=mesh['row'=16,'col'=16] {'row'}, dimensions={0} | all-to-all | bytes 524288 | tf_op jit(solution)/shard_map/all_to_all | solution.py:268
  48.0 2.1 %collective-permute-done.5.other_ref = f32[1280,128]{1,0:T(8,128)S(1)} collective-permute-done((f32[1280,128]{1,0:T(8,128)S(1)}, f32[1280,128]{1,0:T(8,128)S(1)}, u32[]{:S(2)}, u32[]{:S(2)}) %collective-permute-start.5) | collective-permute-done | bytes 655392 | tf_op jit(solution)/shard_map/ppermute | solution.py:296
  50.1 3.2 %wide.1 = f32[256,1024]{1,0:T(8,128)} custom-call(s32[1]{0:T(128)} %bitcast.column, f32[1280,128]{1,0:T(8,128)S(1)} %add_add_fusion.mine_ref, f32[1280,128]{1,0:T(8,128)S(1)} %collective-permute-done.5.other_ref, bf16[1280,1024]{1,0:T(8,128)(2,1)S(1)} %copy-done.1, bf16[1280,1024]{1,0:T(8,128)(2,1)S(1)} %copy-done.2), custom_call_target="tpu_custom_call" | custom-call | flops 6000000000 | bytes 6000000 | tf_op jit(solution)/shard_map/wide/pallas_call | solution.py:229
  53.3 5.9 %all-to-all-start.2 = ((f32[16,16,1024]{2,1,0:T(8,128)}), f32[16,16,1024]{2,1,0:T(8,128)S(1)}, u32[]{:S(2)}, u32[]{:S(2)}) async-start(f32[16,16,1024]{2,1,0:T(8,128)} %bitcast.7), calls=%async_computation.2 | async-start | bytes 2097152 | tf_op jit(solution)/shard_map/all_to_all | solution.py:268
  59.2 11.2 %factor.1 = f32[3,128,128]{2,1,0:T(8,128)S(1)} custom-call(s32[1]{0:T(128)} %bitcast.column, f32[256,256]{1,0:T(8,128)S(1)} %bitcast.22), custom_call_target="tpu_custom_call" | custom-call | flops 12000000000 | bytes 12000000 | tf_op jit(solution)/shard_map/factor/pallas_call | solution.py:229
  70.5 5.4 %collective-permute-start.7 = (f32[3,128,128]{2,1,0:T(8,128)S(1)}, f32[3,128,128]{2,1,0:T(8,128)S(1)}, u32[]{:S(2)}, u32[]{:S(2)}) collective-permute-start(f32[3,128,128]{2,1,0:T(8,128)S(1)} %factor.1), channel_id=1, source_target_pairs={{0,10},{1,11},{16,26},{17,27},{32,42},{33,43},{48,58},{49,59},{64,... | collective-permute-start | bytes 589832 | tf_op jit(solution)/shard_map/ppermute | solution.py:251
  75.9 1.4 %collective-permute-start.6 = (f32[3,128,128]{2,1,0:T(8,128)S(1)}, f32[3,128,128]{2,1,0:T(8,128)S(1)}, u32[]{:S(2)}, u32[]{:S(2)}) collective-permute-start(f32[3,128,128]{2,1,0:T(8,128)S(1)} %factor.1), channel_id=1, source_target_pairs={{0,6},{1,7},{16,22},{17,23},{32,38},{33,39},{48,54},{49,55},{64,70... | collective-permute-start | bytes 589832 | tf_op jit(solution)/shard_map/ppermute | solution.py:251
  78.4 7.2 %all-to-all-start.3 = ((f32[16,16,1024]{2,1,0:T(8,128)}), f32[16,16,1024]{2,1,0:T(8,128)}, u32[]{:S(2)}, u32[]{:S(2)}) async-start(f32[16,16,1024]{2,1,0:T(8,128)} %bitcast.9), calls=%async_computation.3 | async-start | bytes 2097152 | tf_op jit(solution)/shard_map/all_to_all | solution.py:268
  85.7 1.3 %collective-permute-start.9 = (f32[3,128,128]{2,1,0:T(8,128)S(1)}, f32[3,128,128]{2,1,0:T(8,128)S(1)}, u32[]{:S(2)}, u32[]{:S(2)}) collective-permute-start(f32[3,128,128]{2,1,0:T(8,128)S(1)} %add_add_fusion.3), channel_id=1, source_target_pairs={{0,14},{1,15},{6,4},{7,5},{16,30},{17,31},{22,20},{23,21},{32,46},... | collective-permute-start | bytes 589832 | tf_op jit(solution)/shard_map/ppermute | solution.py:251
  87.0 1.5 %collective-permute-start.8 = (f32[3,128,128]{2,1,0:T(8,128)S(1)}, f32[3,128,128]{2,1,0:T(8,128)S(1)}, u32[]{:S(2)}, u32[]{:S(2)}) collective-permute-start(f32[3,128,128]{2,1,0:T(8,128)S(1)} %add_add_fusion.3), channel_id=1, source_target_pairs={{0,2},{1,3},{6,8},{7,9},{10,12},{11,13},{16,18},{17,19},{22,24},{2... | collective-permute-start | bytes 589832 | tf_op jit(solution)/shard_map/ppermute | solution.py:251
  88.5 1.8 %collective-permute-done.9 = f32[3,128,128]{2,1,0:T(8,128)S(1)} collective-permute-done((f32[3,128,128]{2,1,0:T(8,128)S(1)}, f32[3,128,128]{2,1,0:T(8,128)S(1)}, u32[]{:S(2)}, u32[]{:S(2)}) %collective-permute-start.9) | collective-permute-done | bytes 196640 | tf_op jit(solution)/shard_map/ppermute | solution.py:251
  90.4 1.3 %collective-permute-done.8 = f32[3,128,128]{2,1,0:T(8,128)S(1)} collective-permute-done((f32[3,128,128]{2,1,0:T(8,128)S(1)}, f32[3,128,128]{2,1,0:T(8,128)S(1)}, u32[]{:S(2)}, u32[]{:S(2)}) %collective-permute-start.8) | collective-permute-done | bytes 196640 | tf_op jit(solution)/shard_map/ppermute | solution.py:251
  94.2 6.8 %all-to-all-done.3 = f32[16,16,1024]{2,1,0:T(8,128)} async-done(((f32[16,16,1024]{2,1,0:T(8,128)}), f32[16,16,1024]{2,1,0:T(8,128)}, u32[]{:S(2)}, u32[]{:S(2)}) %all-to-all-start.3) | async-done | bytes 1048608 | tf_op jit(solution)/shard_map/all_to_all | solution.py:268
  101.0 7.6 %finish.1 = (f32[10240,128]{1,0:T(8,128)}, f32[2048,128]{1,0:T(8,128)}) custom-call(s32[1]{0:T(128)} %bitcast.column, bf16[1280,256]{1,0:T(8,128)(2,1)} %copy-done.3, bf16[1280,256]{1,0:T(8,128)(2,1)} %copy-done.4, f32[10240,128]{1,0:T(8,128)} %bitcast.25, f32[256,1024]{1,0:T(8,128)} %bitcast.10.w_in, f32[3,128,128]{2,1,0:T(8,128)} %copy-done), custom_call_target="tpu_custom_call" | custom-call | flops 6000000000 | bytes 6000000 | tf_op jit(solution)/shard_map/finish/pallas_call | solution.py:229
  (26 shorter events, 4.4 us)
Async XLA Ops:
  3.4 4.0 %collective-permute-start = (f32[1280,128]{1,0:T(8,128)S(1)}, f32[1280,128]{1,0:T(8,128)S(1)}, u32[]{:S(2)}, u32[]{:S(2)}) collective-permute-start(f32[1280,128]{1,0:T(8,128)S(1)} %bitcast.15), channel_id=1, source_target_pairs={{0,1},{1,0},{16,17},{17,16},{32,33},{33,32},{48,49},{49,48},{64,65... | collective-permute-start | bytes 1966088 | tf_op jit(solution)/shard_map/ppermute | solution.py:281
  9.4 20.3 %collective-permute-start.2 = (f32[1280,128]{1,0:T(8,128)S(1)}, f32[1280,128]{1,0:T(8,128)S(1)}, u32[]{:S(2)}, u32[]{:S(2)}) collective-permute-start(f32[1280,128]{1,0:T(8,128)S(1)} %bitcast.17), channel_id=1, source_target_pairs={{0,10},{1,11},{16,26},{17,27},{32,42},{33,43},{48,58},{49,59},{64,... | collective-permute-start | bytes 1966088 | tf_op jit(solution)/shard_map/ppermute | solution.py:251
  14.8 15.3 %collective-permute-start.1 = (f32[1280,128]{1,0:T(8,128)S(1)}, f32[1280,128]{1,0:T(8,128)S(1)}, u32[]{:S(2)}, u32[]{:S(2)}) collective-permute-start(f32[1280,128]{1,0:T(8,128)S(1)} %bitcast.18), channel_id=1, source_target_pairs={{0,6},{1,7},{16,22},{17,23},{32,38},{33,39},{48,54},{49,55},{64,70... | collective-permute-start | bytes 1966088 | tf_op jit(solution)/shard_map/ppermute | solution.py:251
  16.2 16.7 %all-to-all-start = ((f32[16,16,256]{2,1,0:T(8,128)}), f32[16,16,256]{2,1,0:T(8,128)S(1)}, u32[]{:S(2)}, u32[]{:S(2)}) async-start(f32[16,16,256]{2,1,0:T(8,128)} %bitcast.3), calls=%async_computation | async-start | bytes 524288 | tf_op jit(solution)/shard_map/all_to_all | solution.py:268
  30.2 17.6 %collective-permute-start.4 = (f32[1280,128]{1,0:T(8,128)S(1)}, f32[1280,128]{1,0:T(8,128)S(1)}, u32[]{:S(2)}, u32[]{:S(2)}) collective-permute-start(f32[1280,128]{1,0:T(8,128)S(1)} %add_add_fusion.1), channel_id=1, source_target_pairs={{0,14},{1,15},{6,4},{7,5},{16,30},{17,31},{22,20},{23,21},{32,46},... | collective-permute-start | bytes 1966088 | tf_op jit(solution)/shard_map/ppermute | solution.py:251
  31.5 16.3 %collective-permute-start.3 = (f32[1280,128]{1,0:T(8,128)S(1)}, f32[1280,128]{1,0:T(8,128)S(1)}, u32[]{:S(2)}, u32[]{:S(2)}) collective-permute-start(f32[1280,128]{1,0:T(8,128)S(1)} %add_add_fusion.1), channel_id=1, source_target_pairs={{0,2},{1,3},{6,8},{7,9},{10,12},{11,13},{16,18},{17,19},{22,24},{2... | collective-permute-start | bytes 1966088 | tf_op jit(solution)/shard_map/ppermute | solution.py:251
  32.9 17.2 %copy-start.1 = (bf16[1280,1024]{1,0:T(8,128)(2,1)S(1)}, bf16[1280,1024]{1,0:T(8,128)(2,1)}, u32[]{:S(2)}) copy-start(bf16[1280,1024]{1,0:T(8,128)(2,1)} %get-tuple-element.24.high_ref) | copy-start | bytes 7864324
  32.9 17.2 %copy-start.2 = (bf16[1280,1024]{1,0:T(8,128)(2,1)S(1)}, bf16[1280,1024]{1,0:T(8,128)(2,1)}, u32[]{:S(2)}) copy-start(bf16[1280,1024]{1,0:T(8,128)(2,1)} %get-tuple-element.25.low_ref) | copy-start | bytes 7864324
  47.9 2.2 %collective-permute-start.5 = (f32[1280,128]{1,0:T(8,128)S(1)}, f32[1280,128]{1,0:T(8,128)S(1)}, u32[]{:S(2)}, u32[]{:S(2)}) collective-permute-start(f32[1280,128]{1,0:T(8,128)S(1)} %add_add_fusion.mine_ref), channel_id=1, source_target_pairs={{0,1},{1,0},{2,3},{3,2},{4,5},{5,4},{6,7},{7,6},{8,9},{9,8},{10,11... | collective-permute-start | bytes 1966088 | tf_op jit(solution)/shard_map/ppermute | solution.py:296
  53.3 24.0 %all-to-all-start.2 = ((f32[16,16,1024]{2,1,0:T(8,128)}), f32[16,16,1024]{2,1,0:T(8,128)S(1)}, u32[]{:S(2)}, u32[]{:S(2)}) async-start(f32[16,16,1024]{2,1,0:T(8,128)} %bitcast.7), calls=%async_computation.2 | async-start | bytes 2097152 | tf_op jit(solution)/shard_map/all_to_all | solution.py:268
  70.5 15.2 %collective-permute-start.7 = (f32[3,128,128]{2,1,0:T(8,128)S(1)}, f32[3,128,128]{2,1,0:T(8,128)S(1)}, u32[]{:S(2)}, u32[]{:S(2)}) collective-permute-start(f32[3,128,128]{2,1,0:T(8,128)S(1)} %factor.1), channel_id=1, source_target_pairs={{0,10},{1,11},{16,26},{17,27},{32,42},{33,43},{48,58},{49,59},{64,... | collective-permute-start | bytes 589832 | tf_op jit(solution)/shard_map/ppermute | solution.py:251
  75.9 9.8 %collective-permute-start.6 = (f32[3,128,128]{2,1,0:T(8,128)S(1)}, f32[3,128,128]{2,1,0:T(8,128)S(1)}, u32[]{:S(2)}, u32[]{:S(2)}) collective-permute-start(f32[3,128,128]{2,1,0:T(8,128)S(1)} %factor.1), channel_id=1, source_target_pairs={{0,6},{1,7},{16,22},{17,23},{32,38},{33,39},{48,54},{49,55},{64,70... | collective-permute-start | bytes 589832 | tf_op jit(solution)/shard_map/ppermute | solution.py:251
  78.4 22.6 %all-to-all-start.3 = ((f32[16,16,1024]{2,1,0:T(8,128)}), f32[16,16,1024]{2,1,0:T(8,128)}, u32[]{:S(2)}, u32[]{:S(2)}) async-start(f32[16,16,1024]{2,1,0:T(8,128)} %bitcast.9), calls=%async_computation.3 | async-start | bytes 2097152 | tf_op jit(solution)/shard_map/all_to_all | solution.py:268
  85.7 4.6 %collective-permute-start.9 = (f32[3,128,128]{2,1,0:T(8,128)S(1)}, f32[3,128,128]{2,1,0:T(8,128)S(1)}, u32[]{:S(2)}, u32[]{:S(2)}) collective-permute-start(f32[3,128,128]{2,1,0:T(8,128)S(1)} %add_add_fusion.3), channel_id=1, source_target_pairs={{0,14},{1,15},{6,4},{7,5},{16,30},{17,31},{22,20},{23,21},{32,46},... | collective-permute-start | bytes 589832 | tf_op jit(solution)/shard_map/ppermute | solution.py:251
  87.0 4.6 %collective-permute-start.8 = (f32[3,128,128]{2,1,0:T(8,128)S(1)}, f32[3,128,128]{2,1,0:T(8,128)S(1)}, u32[]{:S(2)}, u32[]{:S(2)}) collective-permute-start(f32[3,128,128]{2,1,0:T(8,128)S(1)} %add_add_fusion.3), channel_id=1, source_target_pairs={{0,2},{1,3},{6,8},{7,9},{10,12},{11,13},{16,18},{17,19},{22,24},{2... | collective-permute-start | bytes 589832 | tf_op jit(solution)/shard_map/ppermute | solution.py:251
  91.7 9.3 %copy-start = (f32[3,128,128]{2,1,0:T(8,128)}, f32[3,128,128]{2,1,0:T(8,128)S(1)}, u32[]{:S(2)}) copy-start(f32[3,128,128]{2,1,0:T(8,128)S(1)} %add_add_fusion.2.x_ref.x_in) | copy-start | bytes 589828
  92.5 0.9 copy-start.3
  93.4 0.8 copy-start.4
